TPU v7x, 256 devices: a whole 4x4x8 slice. The times are simulated.
256 devices in a mesh: ctx: 64 (over z, x, y_hi), fft: 4 (over y_lo, core).
Axes of the slice: x: 4, y: 4 (y_hi: 2, y_lo: 2; y = y_hi * 2 + y_lo), z: 8, core: 2. Of those that a mesh axis runs over, the one named last changes fastest.
Arguments:
- tokens: bfloat16 [32768, 2048], P('ctx'), may hold values from -6 to 6
- w_in: bfloat16 [2048, 3, 2048], P(None, None, 'fft'), may hold values from -0.125 to 0.125
- short_taps: float32 [7, 384], replicated, may hold values from -2 to 2
- long_filter: float32 [32768, 128], P('ctx'), may hold values from -0.03125 to 0.03125
- skip_gain: float32 [2048], replicated, may hold values from -4 to 4
- w_out: bfloat16 [2048, 2048], P('fft'), may hold values from -0.125 to 0.125
Outputs:
- mixed: bfloat16 [32768, 2048], P(('ctx', 'fft'))
All inputs are finite; a program needn't handle non-finite values.
Results may differ from a plain program's by a relative error of at most 0.014.
Values may be sent and summed in bfloat16 or wider, within the bound.
A program may use at most 128 MiB of HBM per device.

v0:
```python
import functools
import math

import jax
import jax.numpy as jnp
import numpy as np
from jax import lax
from jax.experimental import pallas as pl
from jax.experimental.pallas import tpu as pltpu
from jax.sharding import PartitionSpec as P

MESH = pl.DeviceIdType.MESH
F32 = jnp.float32
BF16 = jnp.bfloat16
RIM = 8


def tables(n_ctx, tok_len, stretch):
    blocks = np.arange(n_ctx)
    lags = np.arange(tok_len)
    odd = 2 * blocks + 1
    angle = (odd[:, None] * blocks[None, :] % (4 * n_ctx)) * (2.0 * math.pi / (4 * n_ctx))
    eye = np.eye(stretch)
    over_blocks = np.concatenate([np.cos(angle), -np.sin(angle)], axis=0)
    spread = np.kron(over_blocks, eye)
    turn = (odd[:, None] * lags[None, :]) * (2.0 * math.pi / (4 * n_ctx * tok_len))
    turns = np.stack([np.cos(turn), -np.sin(turn)])
    inner = (lags[:, None] * lags[None, :] % tok_len) * (2.0 * math.pi / tok_len)
    waves = np.concatenate([np.cos(inner), np.sin(inner)], axis=0)
    return (
        over_blocks.astype(np.float32),
        spread.astype(np.float32).astype(jnp.bfloat16),
        turns.astype(np.float32),
        waves.astype(np.float32).astype(jnp.bfloat16),
    )


def dot(a, b, **kw):
    return jnp.dot(a, b, preferred_element_type=F32, **kw)


def kernel(
    n_ctx, n_fft, group_size,
    tok_hbm, w_hbm, taps_hbm, filt_hbm, gain_hbm, wout_hbm, over_hbm, spread_hbm, turns_hbm, waves_hbm,
    out_ref,
    tok, w, taps_in, filt, gain_in, wout, over, spread, turns, waves,
    spread_t, proj, mixed, query, send, recv, filt_send, filt_recv,
    signal, stage, lhs, spec, back, send2, recv2, gated, kept,
    pair_send, pair_recv, cross_send, cross_recv,
    load_sem, rim_send_sem, rim_recv_sem, filt_send_sem, filt_recv_sem,
    go_send_sem, go_recv_sem, come_send_sem, come_recv_sem,
    pair_send_sem, pair_recv_sem, cross_send_sem, cross_recv_sem, own_sem,
):
    me = lax.axis_index("ctx")
    fft = lax.axis_index("fft")
    chip = fft // 2
    core = fft % 2
    partner = chip * 2 + (1 - core)
    across = (1 - chip) * 2 + core
    tok_len, width = tok.shape
    block = w.shape[2]
    stretch = block // n_ctx
    rows = n_ctx * stretch
    n_taps = taps_in.shape[0]
    piece = tok_len // n_fft
    tc = min(128, tok_len)
    lc = min(128, block)
    per_lc = lc // stretch

    barrier = pltpu.get_barrier_semaphore()

    @pl.loop(1, n_ctx)
    def _(i):
        pl.semaphore_signal(barrier, inc=1, device_id={"ctx": lax.rem(me + i, n_ctx)}, device_id_type=MESH)

    for other in (partner, across):
        pl.semaphore_signal(barrier, inc=1, device_id={"fft": other}, device_id_type=MESH)

    loads = {}
    for slot, (name, src, dst) in enumerate([
        ("filt", filt_hbm, filt), ("tok", tok_hbm, tok), ("w1", w_hbm.at[1], w.at[1]), ("w2", w_hbm.at[2], w.at[2]),
        ("taps", taps_hbm, taps_in), ("gain", gain_hbm, gain_in), ("w0", w_hbm.at[0], w.at[0]),
        ("over", over_hbm, over), ("spread", spread_hbm, spread), ("turns", turns_hbm, turns),
        ("waves", waves_hbm, waves), ("wout", wout_hbm, wout),
    ]):
        loads[name] = pltpu.make_async_copy(src, dst, load_sem.at[slot])
        loads[name].start()

    loads["filt"].wait()
    flipped = filt[...].T
    for g in range(flipped.shape[0]):
        filt_send[g, 0, :] = flipped[g, :]

    pl.semaphore_wait(barrier, n_ctx - 1 + 2)

    first_group = fft * (block // group_size)

    def filt_copy(dest):
        return pltpu.make_async_remote_copy(
            src_ref=filt_send.at[first_group + (dest * stretch) // group_size],
            dst_ref=filt_recv.at[me],
            send_sem=filt_send_sem.at[dest], recv_sem=filt_recv_sem.at[me],
            device_id={"ctx": dest}, device_id_type=MESH,
        )

    def filt_arrival(src):
        return pltpu.make_async_remote_copy(
            src_ref=filt_send.at[0], dst_ref=filt_recv.at[src],
            send_sem=filt_send_sem.at[src], recv_sem=filt_recv_sem.at[src],
            device_id={"ctx": src}, device_id_type=MESH,
        )

    @pl.loop(1, n_ctx)
    def _(i):
        filt_copy(lax.rem(me + i, n_ctx)).start()

    own_filt = pltpu.make_async_copy(
        filt_send.at[first_group + (me * stretch) // group_size], filt_recv.at[me], own_sem.at[0])
    own_filt.start()

    def project(s):
        for n0 in range(0, block, min(256, block)):
            n1 = n0 + min(256, block)
            got = dot(tok[...], w[s, :, n0:n1])
            proj[s, RIM:, n0:n1] = got.astype(BF16).astype(F32)

    def rim_copy(s):
        return pltpu.make_async_remote_copy(
            src_ref=proj.at[s, pl.ds(tok_len, RIM), :], dst_ref=proj.at[s, pl.ds(0, RIM), :],
            send_sem=rim_send_sem.at[s], recv_sem=rim_recv_sem.at[s],
            device_id={"ctx": lax.rem(me + 1, n_ctx)}, device_id_type=MESH,
        )

    def send_rim(s):
        @pl.when(me < n_ctx - 1)
        def _():
            rim_copy(s).start()

        @pl.when(me == 0)
        def _():
            proj[s, 0:RIM, :] = jnp.zeros((RIM, block), F32)

    def finish_rim(s):
        @pl.when(me > 0)
        def _():
            rim_copy(s).wait_recv()

    loads["tok"].wait()
    for s, name in ((1, "w1"), (2, "w2")):
        loads[name].wait()
        project(s)
        send_rim(s)

    loads["taps"].wait()
    group_of = lax.broadcasted_iota(jnp.int32, (taps_in.shape[1], block), 1) // group_size
    group_at = lax.broadcasted_iota(jnp.int32, (taps_in.shape[1], block), 0)
    per_stream = taps_in.shape[1] // 3
    taps_of = []
    for s in range(3):
        pick = (group_at == group_of + (s * per_stream + first_group)).astype(F32)
        taps_of.append(dot(taps_in[...], pick, precision=lax.Precision.HIGHEST))

    def featurize(s, t0, c0):
        window = proj[s, pl.ds(t0, tc + RIM), c0:c0 + lc]
        total = None
        for j in range(n_taps):
            term = taps_of[s][j:j + 1, c0:c0 + lc] * window[RIM - j:RIM - j + tc, :]
            total = term if total is None else total + term
        return total.astype(BF16).astype(F32)

    def mix(t0, c0):
        both = featurize(1, t0, c0) * featurize(2, t0, c0)
        mixed[pl.ds(t0, tc), c0:c0 + lc] = both
        turned = both.T.reshape(per_lc, stretch, tc).astype(BF16)
        send[c0 // stretch:c0 // stretch + per_lc, :, pl.ds(t0, tc)] = turned

    for c0 in range(0, block, lc):
        @pl.loop(1, tok_len // tc)
        def _(t):
            mix(pl.multiple_of(t * tc, tc), c0)

    finish_rim(1)
    finish_rim(2)
    for c0 in range(0, block, lc):
        mix(0, c0)

    def swap(source, target, send_sem, recv_sem):
        def outgoing(dest):
            return pltpu.make_async_remote_copy(
                src_ref=source.at[dest], dst_ref=target.at[me],
                send_sem=send_sem.at[dest], recv_sem=recv_sem.at[me],
                device_id={"ctx": dest}, device_id_type=MESH,
            )

        def incoming(src):
            return pltpu.make_async_remote_copy(
                src_ref=source.at[src], dst_ref=target.at[src],
                send_sem=send_sem.at[src], recv_sem=recv_sem.at[src],
                device_id={"ctx": src}, device_id_type=MESH,
            )

        return outgoing, incoming

    go_out, go_in = swap(send, recv, go_send_sem, go_recv_sem)

    @pl.loop(1, n_ctx)
    def _(i):
        go_out(lax.rem(me + i, n_ctx)).start()

    own_go = pltpu.make_async_copy(send.at[me], recv.at[me], own_sem.at[1])
    own_go.start()

    loads["w0"].wait()
    project(0)
    send_rim(0)
    loads["spread"].wait()
    spread_t[...] = spread[...].T

    loads["over"].wait()
    loads["turns"].wait()
    loads["waves"].wait()
    own_filt.wait()

    @pl.loop(1, n_ctx)
    def _(i):
        filt_arrival(lax.rem(me + i, n_ctx)).wait_recv()

    lags = filt_recv[:, 0, :].astype(BF16)
    first = dot(over[...].astype(BF16), lags)
    f_re, f_im = first[:n_ctx], first[n_ctx:]
    t_re, t_im = turns[0], turns[1]
    g_re = (f_re * t_re - f_im * t_im).astype(BF16)
    g_im = (f_re * t_im + f_im * t_re).astype(BF16)
    top = jnp.concatenate([g_re, g_im], axis=1)
    bottom = jnp.concatenate([g_im, -g_re], axis=1)
    scale = 1.0 / (n_ctx * tok_len)
    spec[0] = dot(top, waves[...]) * scale
    spec[1] = dot(bottom, waves[...]) * scale

    finish_rim(0)
    loads["gain"].wait()

    for c0 in range(0, block, lc):
        @pl.loop(0, tok_len // tc)
        def _(t):
            t0 = pl.multiple_of(t * tc, tc)
            query[pl.ds(t0, tc), c0:c0 + lc] = featurize(0, t0, c0)

    own_go.wait()

    @pl.loop(1, n_ctx)
    def _(i):
        go_in(lax.rem(me + i, n_ctx)).wait_recv()

    kc = min(8, n_ctx)
    kr = kc * stretch

    @pl.loop(0, n_ctx // kc)
    def _(i):
        got = recv[pl.ds(i * kc, kc)].astype(F32)
        signal[pl.ds(pl.multiple_of(i * kr, kr), kr), :] = got.reshape(kr, tok_len).astype(BF16)

    mc = min(256, rows)
    lt = min(128, tok_len)

    for m0 in range(0, 2 * rows, mc):
        stage[m0:m0 + mc, :] = dot(spread[m0:m0 + mc, :], signal[...])

    def pieces(i, n0, table):
        k0 = pl.multiple_of(i * kr, kr)
        re = stage[pl.ds(k0, kr), n0:n0 + lt].reshape(kc, stretch, lt)
        im = stage[pl.ds(rows + k0, kr), n0:n0 + lt].reshape(kc, stretch, lt)
        b_re = table[0, pl.ds(pl.multiple_of(i * kc, kc), kc), n0:n0 + lt][:, None, :]
        b_im = table[1, pl.ds(pl.multiple_of(i * kc, kc), kc), n0:n0 + lt][:, None, :]
        return k0, re, im, b_re, b_im

    @pl.loop(0, n_ctx // kc)
    def _(i):
        for n0 in range(0, tok_len, lt):
            k0, re, im, b_re, b_im = pieces(i, n0, turns)
            o_re = (re * b_re - im * b_im).reshape(kr, lt)
            o_im = (re * b_im + im * b_re).reshape(kr, lt)
            lhs[pl.ds(k0, kr), n0:n0 + lt] = o_re.astype(BF16)
            lhs[pl.ds(k0, kr), tok_len + n0:tok_len + n0 + lt] = o_im.astype(BF16)
            lhs[pl.ds(rows + k0, kr), n0:n0 + lt] = o_im.astype(BF16)
            lhs[pl.ds(rows + k0, kr), tok_len + n0:tok_len + n0 + lt] = (-o_re).astype(BF16)

    for m0 in range(0, 2 * rows, mc):
        stage[m0:m0 + mc, :] = dot(lhs[m0:m0 + mc, :], waves[...])

    @pl.loop(0, n_ctx // kc)
    def _(i):
        for n0 in range(0, tok_len, lt):
            k0, re, im, b_re, b_im = pieces(i, n0, spec)
            o_re = (re * b_re - im * b_im).reshape(kr, lt)
            o_im = (re * b_im + im * b_re).reshape(kr, lt)
            lhs[pl.ds(k0, kr), n0:n0 + lt] = o_re.astype(BF16)
            lhs[pl.ds(k0, kr), tok_len + n0:tok_len + n0 + lt] = (-o_im).astype(BF16)
            lhs[pl.ds(rows + k0, kr), n0:n0 + lt] = o_im.astype(BF16)
            lhs[pl.ds(rows + k0, kr), tok_len + n0:tok_len + n0 + lt] = o_re.astype(BF16)

    for m0 in range(0, 2 * rows, mc):
        stage[m0:m0 + mc, :] = dot(lhs[m0:m0 + mc, :], waves[...])

    @pl.loop(0, n_ctx // kc)
    def _(i):
        for n0 in range(0, tok_len, lt):
            k0, re, im, b_re, b_im = pieces(i, n0, turns)
            o_re = (re * b_re + im * b_im).reshape(kr, lt)
            o_im = (im * b_re - re * b_im).reshape(kr, lt)
            back[pl.ds(k0, kr), n0:n0 + lt] = o_re.astype(BF16)
            back[pl.ds(rows + k0, kr), n0:n0 + lt] = o_im.astype(BF16)

    for m0 in range(0, rows, mc):
        got = dot(spread_t[m0:m0 + mc, :], back[...])
        send2[m0 // stretch:(m0 + mc) // stretch] = got.reshape(mc // stretch, stretch, tok_len).astype(BF16)

    come_out, come_in = swap(send2, recv2, come_send_sem, come_recv_sem)

    @pl.loop(1, n_ctx)
    def _(i):
        come_out(lax.rem(me + i, n_ctx)).start()

    own_come = pltpu.make_async_copy(send2.at[me], recv2.at[me], own_sem.at[2])
    own_come.start()

    loads["wout"].wait()
    own_come.wait()

    @pl.loop(1, n_ctx)
    def _(i):
        come_in(lax.rem(me + i, n_ctx)).wait_recv()

    gain_row = gain_in[:, pl.ds(pl.multiple_of(fft * block, block), block)]
    for c0 in range(0, block, lc):
        @pl.loop(0, tok_len // tc)
        def _(t):
            t0 = pl.multiple_of(t * tc, tc)
            got = recv2[c0 // stretch:c0 // stretch + per_lc, :, pl.ds(t0, tc)].astype(F32)
            conv = got.reshape(lc, tc).T
            whole = conv + gain_row[:, c0:c0 + lc] * mixed[pl.ds(t0, tc), c0:c0 + lc]
            gated[pl.ds(t0, tc), c0:c0 + lc] = (query[pl.ds(t0, tc), c0:c0 + lc] * whole).astype(BF16)

    oc = min(512, width)

    def partial(owner, n0):
        return dot(gated[pl.ds(pl.multiple_of(owner * piece, piece), piece), :], wout[:, n0:n0 + oc])

    def pair_copy(i):
        return pltpu.make_async_remote_copy(
            src_ref=pair_send.at[i], dst_ref=pair_recv.at[i],
            send_sem=pair_send_sem.at[i], recv_sem=pair_recv_sem.at[i],
            device_id={"fft": partner}, device_id_type=MESH,
        )

    cross_copy = pltpu.make_async_remote_copy(
        src_ref=cross_send, dst_ref=cross_recv, send_sem=cross_send_sem, recv_sem=cross_recv_sem,
        device_id={"fft": across}, device_id_type=MESH,
    )

    for i, owner in ((0, (1 - chip) * 2 + (1 - core)), (1, partner)):
        for n0 in range(0, width, oc):
            pair_send[i, :, n0:n0 + oc] = partial(owner, n0).astype(BF16)
        pair_copy(i).start()

    for n0 in range(0, width, oc):
        kept[:, n0:n0 + oc] = partial(across, n0)
    pair_copy(0).wait_recv()
    for n0 in range(0, width, oc):
        cross_send[:, n0:n0 + oc] = (kept[:, n0:n0 + oc] + pair_recv[0, :, n0:n0 + oc].astype(F32)).astype(BF16)
    cross_copy.start()
    for n0 in range(0, width, oc):
        kept[:, n0:n0 + oc] = partial(fft, n0)
    pair_copy(1).wait_recv()
    for n0 in range(0, width, oc):
        kept[:, n0:n0 + oc] = kept[:, n0:n0 + oc] + pair_recv[1, :, n0:n0 + oc].astype(F32)
    cross_copy.wait_recv()
    for n0 in range(0, width, oc):
        out_ref[:, n0:n0 + oc] = (kept[:, n0:n0 + oc] + cross_recv[:, n0:n0 + oc].astype(F32)).astype(BF16)

    pair_copy(0).wait_send()
    pair_copy(1).wait_send()
    cross_copy.wait_send()

    @pl.when(me < n_ctx - 1)
    def _():
        for s in range(3):
            rim_copy(s).wait_send()

    @pl.loop(1, n_ctx)
    def _(i):
        dest = lax.rem(me + i, n_ctx)
        filt_copy(dest).wait_send()
        go_out(dest).wait_send()
        come_out(dest).wait_send()


def body(tokens, w_in, short_taps, long_filter, skip_gain, w_out):
    n_ctx = lax.axis_size("ctx")
    n_fft = lax.axis_size("fft")
    tok_len, width = tokens.shape
    block = w_in.shape[2]
    n_groups = long_filter.shape[1]
    group_size = width // n_groups
    stretch = block // n_ctx
    rows = n_ctx * stretch
    piece = tok_len // n_fft
    over, spread, turns, waves = tables(n_ctx, tok_len, stretch)
    dma = pltpu.SemaphoreType.DMA
    vmem = pltpu.VMEM
    streams = w_in.transpose(1, 0, 2)
    args = (
        tokens, streams, short_taps, long_filter, skip_gain.reshape(1, width), w_out,
        jnp.asarray(over), jnp.asarray(spread), jnp.asarray(turns), jnp.asarray(waves),
    )
    return pl.pallas_call(
        functools.partial(kernel, n_ctx, n_fft, group_size),
        out_shape=jax.ShapeDtypeStruct((piece, width), BF16),
        in_specs=[pl.BlockSpec(memory_space=pl.ANY)] * len(args),
        out_specs=pl.BlockSpec(memory_space=vmem),
        scratch_shapes=[vmem(a.shape, a.dtype) for a in args] + [
            vmem((rows, 2 * rows), BF16),
            vmem((3, tok_len + RIM, block), F32),
            vmem((tok_len, block), F32),
            vmem((tok_len, block), F32),
            vmem((n_ctx, stretch, tok_len), BF16),
            vmem((n_ctx, stretch, tok_len), BF16),
            vmem((n_groups, 1, tok_len), F32),
            vmem((n_ctx, 1, tok_len), F32),
            vmem((rows, tok_len), BF16),
            vmem((2 * rows, tok_len), F32),
            vmem((2 * rows, 2 * tok_len), BF16),
            vmem((2, n_ctx, tok_len), F32),
            vmem((2 * rows, tok_len), BF16),
            vmem((n_ctx, stretch, tok_len), BF16),
            vmem((n_ctx, stretch, tok_len), BF16),
            vmem((tok_len, block), BF16),
            vmem((piece, width), F32),
            vmem((2, piece, width), BF16),
            vmem((2, piece, width), BF16),
            vmem((piece, width), BF16),
            vmem((piece, width), BF16),
            dma((12,)), dma((3,)), dma((3,)),
            dma((n_ctx,)), dma((n_ctx,)), dma((n_ctx,)), dma((n_ctx,)), dma((n_ctx,)), dma((n_ctx,)),
            dma((2,)), dma((2,)), dma, dma, dma((3,)),
        ],
        compiler_params=pltpu.CompilerParams(
            collective_id=0, has_side_effects=True, vmem_limit_bytes=60 * 1024 * 1024
        ),
        name="hyena",
    )(*args)


def solution(mesh):
    return jax.shard_map(
        body,
        mesh=mesh,
        in_specs=(P("ctx", None), P(None, None, "fft"), P(), P("ctx", None), P(), P("fft", None)),
        out_specs=P(("ctx", "fft"), None),
        check_vma=False,
    )
```

profile of v0, /device:TPU:1, one launch (start us, length us, event | category | flops | bytes accessed | tf_op | source)
XLA Modules:
  0.0 83.1 jit_solution(2264942241846371178)
XLA Ops:
  0.0 81.2 %hyena.1 = bf16[128,2048]{1,0:T(8,128)(2,1)} custom-call(bf16[512,2048]{1,0:T(8,128)(2,1)} %tok_hbm.1, bf16[3,2048,512]{2,1,0:T(8,128)(2,1)} %bitcast.2, f32[7,384]{1,0:T(8,128)} %taps_hbm.1, f32[512,128]{1,0:T(8,128)} %filt_hbm.1, f32[1,2048]{1,0:T(1,128)} %bitcast.3, bf16[512,2048]{1,0:T(8,128)(2,1)} %wout_hbm.1, f32[128,64]{1,0:T(8,128)} %constant.8.clone.over_hbm, ...), custom_call_target="tpu_custom_call" | custom-call | tf_op jit(solution)/shard_map/hyena/pallas_call | solution.py:416
  81.2 1.9 %copy.12 = bf16[128,2048]{1,0:T(8,128)(2,1)} copy(bf16[128,2048]{1,0:T(8,128)(2,1)} %hyena.1) | data formatting | bytes 1048576
where the time goes:
time: 83.2 us; the launch traced here: 83.1 us
  Pallas kernels  81.2 us (98%)
  local copies, waits for them, and re-layouts  1.88 us (2%)
    pallas_call x1, Pallas kernels, body(): pl.pallas_call(functools.partial(kernel, n_ctx, n_fft, group_size), out_s...  81.2 us
    unnamed x1, local copies, waits for them, and re-layouts  1.88 us

commit v1 on v0

v1 whole, which is shorter than its diff:
```python
import functools
import math

import jax
import jax.numpy as jnp
import numpy as np
from jax import lax
from jax.experimental import pallas as pl
from jax.experimental.pallas import tpu as pltpu
from jax.sharding import PartitionSpec as P

MESH = pl.DeviceIdType.MESH
F32 = jnp.float32
BF16 = jnp.bfloat16
RIM = 8


def tables(n_ctx, tok_len, stretch):
    blocks = np.arange(n_ctx)
    lags = np.arange(tok_len)
    odd = 2 * blocks + 1
    angle = (odd[:, None] * blocks[None, :] % (4 * n_ctx)) * (2.0 * math.pi / (4 * n_ctx))
    eye = np.eye(stretch)
    over_blocks = np.concatenate([np.cos(angle), -np.sin(angle)], axis=0)
    spread = np.kron(over_blocks, eye)
    turn = (odd[:, None] * lags[None, :]) * (2.0 * math.pi / (4 * n_ctx * tok_len))
    turns = np.stack([np.cos(turn), -np.sin(turn)])
    inner = (lags[:, None] * lags[None, :] % tok_len) * (2.0 * math.pi / tok_len)
    waves = np.concatenate([np.cos(inner), np.sin(inner)], axis=0)
    return (
        over_blocks.astype(np.float32),
        spread.astype(np.float32).astype(jnp.bfloat16),
        turns.astype(np.float32),
        waves.astype(np.float32).astype(jnp.bfloat16),
    )


def dot(a, b, **kw):
    return jnp.dot(a, b, preferred_element_type=F32, **kw)


def kernel(
    n_ctx, n_fft, group_size,
    tok_hbm, w_hbm, taps_hbm, filt_hbm, gain_hbm, wout_hbm, over_hbm, spread_hbm, turns_hbm, waves_hbm,
    out_ref,
    tok, w, taps_in, filt, gain_in, wout, over, spread, turns, waves,
    spread_t, proj, mixed, query, send, recv, filt_send, filt_recv,
    signal, stage, lhs, spec, back, send2, recv2, gated, part, kept,
    pair_send, pair_recv, cross_send, cross_recv,
    load_sem, rim_send_sem, rim_recv_sem, filt_sem, go_send_sem, go_recv_sem, come_send_sem, come_recv_sem,
    pair_send_sem, pair_recv_sem, cross_send_sem, cross_recv_sem,
):
    me = lax.axis_index("ctx")
    fft = lax.axis_index("fft")
    chip = fft // 2
    core = fft % 2
    partner = chip * 2 + (1 - core)
    across = (1 - chip) * 2 + core
    tok_len, width = tok.shape
    block = w.shape[2]
    stretch = block // n_ctx
    rows = n_ctx * stretch
    n_taps = taps_in.shape[0]
    piece = tok_len // n_fft
    half = tok_len // 2
    tc = min(128, half)
    lc = min(128, block)
    per_lc = lc // stretch

    barrier = pltpu.get_barrier_semaphore()

    def each_peer(act):
        @pl.loop(1, n_ctx)
        def _(i):
            m = n_ctx - i
            d = (m + 1) // 2
            odd = m % 2
            act(lax.rem(me + odd * d + (1 - odd) * (n_ctx - d), n_ctx))

    each_peer(lambda peer: pl.semaphore_signal(barrier, inc=1, device_id={"ctx": peer}, device_id_type=MESH))
    for other in (partner, across):
        pl.semaphore_signal(barrier, inc=1, device_id={"fft": other}, device_id_type=MESH)

    split = half - 16
    loads = {}
    for slot, (name, src, dst) in enumerate([
        ("taps", taps_hbm, taps_in),
        ("tok1", tok_hbm.at[pl.ds(split, tok_len - split)], tok.at[pl.ds(split, tok_len - split)]),
        ("w1", w_hbm.at[1], w.at[1]), ("w2", w_hbm.at[2], w.at[2]),
        ("tok0", tok_hbm.at[pl.ds(0, split)], tok.at[pl.ds(0, split)]),
        ("filt", filt_hbm, filt), ("w0", w_hbm.at[0], w.at[0]), ("gain", gain_hbm, gain_in),
        ("spread", spread_hbm, spread), ("over", over_hbm, over), ("turns", turns_hbm, turns),
        ("waves", waves_hbm, waves), ("wout", wout_hbm, wout),
    ]):
        loads[name] = pltpu.make_async_copy(src, dst, load_sem.at[slot])
        loads[name].start()

    first_group = fft * (block // group_size)
    per_stream = taps_in.shape[1] // 3
    loads["taps"].wait()
    group_of = lax.broadcasted_iota(jnp.int32, (per_stream, block), 1) // group_size + first_group
    pick = (lax.broadcasted_iota(jnp.int32, (per_stream, block), 0) == group_of).astype(F32)
    blank = jnp.zeros((8 - n_taps, per_stream), F32)
    taps_rows = jnp.concatenate(
        [x for s in range(3) for x in (taps_in[:, s * per_stream:(s + 1) * per_stream], blank)], axis=0
    )
    taps_all = dot(taps_rows, pick, precision=lax.Precision.HIGHEST)

    def project(s, r0, r1):
        for n0 in range(0, block, min(256, block)):
            n1 = n0 + min(256, block)
            got = dot(tok[r0:r1, :], w[s, :, n0:n1])
            proj[s, RIM + r0:RIM + r1, n0:n1] = got.astype(BF16).astype(F32)

    def rim_copy(s):
        return pltpu.make_async_remote_copy(
            src_ref=proj.at[s, pl.ds(tok_len, RIM), :], dst_ref=proj.at[s, pl.ds(0, RIM), :],
            send_sem=rim_send_sem.at[s], recv_sem=rim_recv_sem.at[s],
            device_id={"ctx": lax.rem(me + 1, n_ctx)}, device_id_type=MESH,
        )

    def send_rim(s):
        @pl.when(me < n_ctx - 1)
        def _():
            rim_copy(s).start()

        @pl.when(me == 0)
        def _():
            proj[s, 0:RIM, :] = jnp.zeros((RIM, block), F32)

    def finish_rim(s):
        @pl.when(me > 0)
        def _():
            rim_copy(s).wait_recv()

    def featurize(s, t0, c0):
        window = proj[s, pl.ds(t0, tc + RIM), c0:c0 + lc]
        total = None
        for j in range(n_taps):
            term = taps_all[s * 8 + j:s * 8 + j + 1, c0:c0 + lc] * window[RIM - j:RIM - j + tc, :]
            total = term if total is None else total + term
        return total.astype(BF16).astype(F32)

    def mix(t0, c0):
        both = featurize(1, t0, c0) * featurize(2, t0, c0)
        mixed[pl.ds(t0, tc), c0:c0 + lc] = both
        turned = both.T.reshape(per_lc, stretch, tc).astype(BF16)
        send[c0 // stretch:c0 // stretch + per_lc, :, pl.ds(t0, tc)] = turned

    def exchange(source, target, send_sem, recv_sem):
        def at(ref, where, h0):
            return ref.at[where, :, pl.ds(h0, half)]

        def copy_to(dest, h0, i):
            return pltpu.make_async_remote_copy(
                src_ref=at(source, dest, h0), dst_ref=at(target, me, h0),
                send_sem=send_sem.at[i], recv_sem=recv_sem.at[i],
                device_id={"ctx": dest}, device_id_type=MESH,
            )

        def start(h0, i):
            each_peer(lambda dest: copy_to(dest, h0, i).start())
            target[me, :, pl.ds(h0, half)] = source[me, :, pl.ds(h0, half)]

        def all_of(h0, i):
            return pltpu.make_async_remote_copy(
                src_ref=at(source, pl.ds(0, n_ctx - 1), h0), dst_ref=at(target, pl.ds(0, n_ctx - 1), h0),
                send_sem=send_sem.at[i], recv_sem=recv_sem.at[i],
                device_id={"ctx": lax.rem(me + 1, n_ctx)}, device_id_type=MESH,
            )

        return start, all_of

    go_start, go_all = exchange(send, recv, go_send_sem, go_recv_sem)

    loads["tok1"].wait()
    for s, name in ((1, "w1"), (2, "w2")):
        loads[name].wait()
        project(s, split, tok_len)
    for c0 in range(0, block, lc):
        @pl.loop(half // tc, tok_len // tc)
        def _(t):
            mix(pl.multiple_of(t * tc, tc), c0)

    pl.semaphore_wait(barrier, n_ctx - 1 + 2)
    send_rim(1)
    send_rim(2)
    go_start(half, 1)

    loads["tok0"].wait()
    project(1, 0, split)
    project(2, 0, split)
    for c0 in range(0, block, lc):
        @pl.loop(1, half // tc)
        def _(t):
            mix(pl.multiple_of(t * tc, tc), c0)

    finish_rim(1)
    finish_rim(2)
    for c0 in range(0, block, lc):
        mix(0, c0)
    go_start(0, 0)

    loads["filt"].wait()
    flipped = filt[...].T.astype(BF16).astype(F32)
    lag_rows, lag_lanes = filt_send.shape[1:]
    for j in range(lag_rows):
        filt_send[:, j, :] = flipped[:, j * lag_lanes:(j + 1) * lag_lanes].astype(BF16)

    def filt_copy(dest):
        return pltpu.make_async_remote_copy(
            src_ref=filt_send.at[first_group + (dest * stretch) // group_size],
            dst_ref=filt_recv.at[me],
            send_sem=filt_sem.at[0], recv_sem=filt_sem.at[1],
            device_id={"ctx": dest}, device_id_type=MESH,
        )

    filt_all = pltpu.make_async_remote_copy(
        src_ref=filt_recv.at[pl.ds(0, n_ctx - 1)], dst_ref=filt_recv.at[pl.ds(0, n_ctx - 1)],
        send_sem=filt_sem.at[0], recv_sem=filt_sem.at[1],
        device_id={"ctx": lax.rem(me + 1, n_ctx)}, device_id_type=MESH,
    )
    each_peer(lambda dest: filt_copy(dest).start())
    filt_recv[me] = filt_send[first_group + (me * stretch) // group_size]

    loads["w0"].wait()
    project(0, 0, tok_len)
    send_rim(0)
    loads["spread"].wait()
    spread_t[...] = spread[...].T
    finish_rim(0)
    for c0 in range(0, block, lc):
        @pl.loop(0, tok_len // tc)
        def _(t):
            t0 = pl.multiple_of(t * tc, tc)
            query[pl.ds(t0, tc), c0:c0 + lc] = featurize(0, t0, c0)

    kc = min(8, n_ctx)
    kr = kc * stretch
    mc = min(256, rows)
    lt = min(128, half)

    def pieces(i, n0, table):
        k0 = pl.multiple_of(i * kr, kr)
        cols = pl.ds(n0, lt)
        re = stage[pl.ds(k0, kr), cols].reshape(kc, stretch, lt)
        im = stage[pl.ds(rows + k0, kr), cols].reshape(kc, stretch, lt)
        b_re = table[0, pl.ds(pl.multiple_of(i * kc, kc), kc), cols][:, None, :]
        b_im = table[1, pl.ds(pl.multiple_of(i * kc, kc), kc), cols][:, None, :]
        return k0, re, im, b_re, b_im

    loads["turns"].wait()

    def first_stage(h0):
        @pl.loop(0, n_ctx // kc)
        def _(i):
            got = recv[pl.ds(i * kc, kc), :, h0:h0 + half].astype(F32)
            signal[pl.ds(pl.multiple_of(i * kr, kr), kr), h0:h0 + half] = got.reshape(kr, half).astype(BF16)

        for m0 in range(0, 2 * rows, mc):
            stage[m0:m0 + mc, h0:h0 + half] = dot(spread[m0:m0 + mc, :], signal[:, h0:h0 + half])

        @pl.loop(0, n_ctx // kc)
        def _(i):
            for n0 in range(h0, h0 + half, lt):
                k0, re, im, b_re, b_im = pieces(i, n0, turns)
                o_re = (re * b_re - im * b_im).reshape(kr, lt)
                o_im = (re * b_im + im * b_re).reshape(kr, lt)
                lhs[pl.ds(k0, kr), n0:n0 + lt] = o_re.astype(BF16)
                lhs[pl.ds(k0, kr), tok_len + n0:tok_len + n0 + lt] = o_im.astype(BF16)
                lhs[pl.ds(rows + k0, kr), n0:n0 + lt] = o_im.astype(BF16)
                lhs[pl.ds(rows + k0, kr), tok_len + n0:tok_len + n0 + lt] = (-o_re).astype(BF16)

    go_all(half, 1).wait_recv()
    first_stage(half)

    loads["over"].wait()
    loads["waves"].wait()
    filt_all.wait_recv()
    lags3 = filt_recv[...].astype(F32)
    lags = jnp.concatenate([lags3[:, j, :] for j in range(lag_rows)], axis=1).astype(BF16)
    first = dot(over[...].astype(BF16), lags)
    f_re, f_im = first[:n_ctx], first[n_ctx:]
    t_re, t_im = turns[0], turns[1]
    g_re = (f_re * t_re - f_im * t_im).astype(BF16)
    g_im = (f_re * t_im + f_im * t_re).astype(BF16)
    top = jnp.concatenate([g_re, g_im], axis=1)
    bottom = jnp.concatenate([g_im, -g_re], axis=1)
    scale = 1.0 / (n_ctx * tok_len)
    spec[0] = dot(top, waves[...]) * scale
    spec[1] = dot(bottom, waves[...]) * scale

    go_all(0, 0).wait_recv()
    first_stage(0)

    for m0 in range(0, 2 * rows, mc):
        stage[m0:m0 + mc, :] = dot(lhs[m0:m0 + mc, :], waves[...])

    @pl.loop(0, n_ctx // kc)
    def _(i):
        for n0 in range(0, tok_len, lt):
            k0, re, im, b_re, b_im = pieces(i, n0, spec)
            o_re = (re * b_re - im * b_im).reshape(kr, lt)
            o_im = (re * b_im + im * b_re).reshape(kr, lt)
            lhs[pl.ds(k0, kr), n0:n0 + lt] = o_re.astype(BF16)
            lhs[pl.ds(k0, kr), tok_len + n0:tok_len + n0 + lt] = (-o_im).astype(BF16)
            lhs[pl.ds(rows + k0, kr), n0:n0 + lt] = o_im.astype(BF16)
            lhs[pl.ds(rows + k0, kr), tok_len + n0:tok_len + n0 + lt] = o_re.astype(BF16)

    come_start, come_all = exchange(send2, recv2, come_send_sem, come_recv_sem)

    def last_stage(h0, i):
        for m0 in range(0, 2 * rows, mc):
            stage[m0:m0 + mc, pl.ds(h0, half)] = dot(lhs[m0:m0 + mc, :], waves[:, pl.ds(h0, half)])

        @pl.loop(0, n_ctx // kc)
        def _(i):
            for j in range(half // lt):
                n0 = pl.multiple_of(h0 + j * lt, lt)
                k0, re, im, b_re, b_im = pieces(i, n0, turns)
                o_re = (re * b_re + im * b_im).reshape(kr, lt)
                o_im = (im * b_re - re * b_im).reshape(kr, lt)
                back[pl.ds(k0, kr), pl.ds(n0, lt)] = o_re.astype(BF16)
                back[pl.ds(rows + k0, kr), pl.ds(n0, lt)] = o_im.astype(BF16)

        for m0 in range(0, rows, mc):
            got = dot(spread_t[m0:m0 + mc, :], back[:, pl.ds(h0, half)])
            send2[m0 // stretch:(m0 + mc) // stretch, :, pl.ds(h0, half)] = (
                got.reshape(mc // stretch, stretch, half).astype(BF16))
        come_start(h0, i)

    theirs = pl.multiple_of((1 - chip) * half, half)
    ours = pl.multiple_of(chip * half, half)
    last_stage(theirs, 0)
    last_stage(ours, 1)

    loads["wout"].wait()
    loads["gain"].wait()
    gain_row = gain_in[:, pl.ds(pl.multiple_of(fft * block, block), block)]
    n_chunks, oc = pair_send.shape[1], pair_send.shape[3]

    def gate(h0):
        for c0 in range(0, block, lc):
            @pl.loop(0, half // tc)
            def _(t):
                t0 = pl.multiple_of(h0 + t * tc, tc)
                got = recv2[c0 // stretch:c0 // stretch + per_lc, :, pl.ds(t0, tc)].astype(F32)
                conv = got.reshape(lc, tc).T
                whole = conv + gain_row[:, c0:c0 + lc] * mixed[pl.ds(t0, tc), c0:c0 + lc]
                gated[pl.ds(t0, tc), c0:c0 + lc] = (query[pl.ds(t0, tc), c0:c0 + lc] * whole).astype(BF16)

    def pair_copy(i, n):
        return pltpu.make_async_remote_copy(
            src_ref=pair_send.at[i, n], dst_ref=pair_recv.at[i, n],
            send_sem=pair_send_sem.at[i, n], recv_sem=pair_recv_sem.at[i, n],
            device_id={"fft": partner}, device_id_type=MESH,
        )

    def cross_copy(n):
        return pltpu.make_async_remote_copy(
            src_ref=cross_send.at[n], dst_ref=cross_recv.at[n],
            send_sem=cross_send_sem.at[n], recv_sem=cross_recv_sem.at[n],
            device_id={"fft": across}, device_id_type=MESH,
        )

    def partials(h0, i):
        for n in range(n_chunks):
            part[n] = dot(gated[pl.ds(h0, half), :], wout[:, n * oc:(n + 1) * oc])
            pair_send[i, n] = part[n, pl.ds(pl.multiple_of((1 - core) * piece, piece), piece), :].astype(BF16)
            pair_copy(i, n).start()

    def pair_sum(i, n):
        pair_copy(i, n).wait_recv()
        return part[n, pl.ds(pl.multiple_of(core * piece, piece), piece), :] + pair_recv[i, n].astype(F32)

    go_all(half, 1).wait_send()
    go_all(0, 0).wait_send()
    filt_all.wait_send()

    @pl.when(me < n_ctx - 1)
    def _():
        for s in range(3):
            rim_copy(s).wait_send()

    come_all(theirs, 0).wait_recv()
    gate(theirs)
    partials(theirs, 0)
    for n in range(n_chunks):
        cross_send[n] = pair_sum(0, n).astype(BF16)
        cross_copy(n).start()

    come_all(ours, 1).wait_recv()
    gate(ours)
    partials(ours, 1)
    for n in range(n_chunks):
        kept[n] = pair_sum(1, n)

    come_all(theirs, 0).wait_send()
    come_all(ours, 1).wait_send()
    for n in range(n_chunks):
        pair_copy(0, n).wait_send()
        pair_copy(1, n).wait_send()
    for n in range(n_chunks):
        cross_copy(n).wait_recv()
        out_ref[:, n * oc:(n + 1) * oc] = (kept[n] + cross_recv[n].astype(F32)).astype(BF16)
    for n in range(n_chunks):
        cross_copy(n).wait_send()


def body(tokens, w_in, short_taps, long_filter, skip_gain, w_out):
    n_ctx = lax.axis_size("ctx")
    n_fft = lax.axis_size("fft")
    tok_len, width = tokens.shape
    block = w_in.shape[2]
    n_groups = long_filter.shape[1]
    group_size = width // n_groups
    stretch = block // n_ctx
    rows = n_ctx * stretch
    piece = tok_len // n_fft
    oc = min(512, width)
    n_chunks = width // oc
    lag_rows = 4
    over, spread, turns, waves = tables(n_ctx, tok_len, stretch)
    dma = pltpu.SemaphoreType.DMA
    vmem = pltpu.VMEM
    streams = w_in.transpose(1, 0, 2)
    args = (
        tokens, streams, short_taps, long_filter, skip_gain.reshape(1, width), w_out,
        jnp.asarray(over), jnp.asarray(spread), jnp.asarray(turns), jnp.asarray(waves),
    )
    return pl.pallas_call(
        functools.partial(kernel, n_ctx, n_fft, group_size),
        out_shape=jax.ShapeDtypeStruct((piece, width), BF16),
        in_specs=[pl.BlockSpec(memory_space=pl.ANY)] * len(args),
        out_specs=pl.BlockSpec(memory_space=vmem),
        scratch_shapes=[vmem(a.shape, a.dtype) for a in args] + [
            vmem((rows, 2 * rows), BF16),
            vmem((3, tok_len + RIM, block), F32),
            vmem((tok_len, block), F32),
            vmem((tok_len, block), F32),
            vmem((n_ctx, stretch, tok_len), BF16),
            vmem((n_ctx, stretch, tok_len), BF16),
            vmem((n_groups, lag_rows, tok_len // lag_rows), BF16),
            vmem((n_ctx, lag_rows, tok_len // lag_rows), BF16),
            vmem((rows, tok_len), BF16),
            vmem((2 * rows, tok_len), F32),
            vmem((2 * rows, 2 * tok_len), BF16),
            vmem((2, n_ctx, tok_len), F32),
            vmem((2 * rows, tok_len), BF16),
            vmem((n_ctx, stretch, tok_len), BF16),
            vmem((n_ctx, stretch, tok_len), BF16),
            vmem((tok_len, block), BF16),
            vmem((n_chunks, tok_len // 2, oc), F32),
            vmem((n_chunks, piece, oc), F32),
            vmem((2, n_chunks, piece, oc), BF16),
            vmem((2, n_chunks, piece, oc), BF16),
            vmem((n_chunks, piece, oc), BF16),
            vmem((n_chunks, piece, oc), BF16),
            dma((13,)), dma((3,)), dma((3,)), dma((2,)), dma((2,)), dma((2,)), dma((2,)), dma((2,)),
            dma((2, n_chunks)), dma((2, n_chunks)), dma((n_chunks,)), dma((n_chunks,)),
        ],
        compiler_params=pltpu.CompilerParams(
            collective_id=0, has_side_effects=True, vmem_limit_bytes=60 * 1024 * 1024
        ),
        name="hyena",
    )(*args)


def solution(mesh):
    return jax.shard_map(
        body,
        mesh=mesh,
        in_specs=(P("ctx", None), P(None, None, "fft"), P(), P("ctx", None), P(), P("fft", None)),
        out_specs=P(("ctx", "fft"), None),
        check_vma=False,
    )
```

time: 83.2 us -> 66.6 us (0.80)
  Pallas kernels: 81.2 us -> 64.5 us
    pallas_call x1, Pallas kernels: 81.2 us -> 64.5 us  [body(): pl.pallas_call(functools.partial(kernel, n_ctx, n_fft, group_size), out_s...]
where the time goes in v1:
time: 66.6 us; the launch traced here: 66.4 us
  Pallas kernels  64.5 us (97%)
  local copies, waits for them, and re-layouts  1.88 us (3%)
    pallas_call x1, Pallas kernels, body(): pl.pallas_call(functools.partial(kernel, n_ctx, n_fft, group_size), out_s...  64.5 us
    unnamed x1, local copies, waits for them, and re-layouts  1.88 us

profile of v1, /device:TPU:1, one launch (start us, length us, event | category | flops | bytes accessed | tf_op | source)
XLA Modules:
  0.0 66.4 jit_solution(8764518385826412056)
XLA Ops:
  0.0 64.5 %hyena.1 = bf16[128,2048]{1,0:T(8,128)(2,1)} custom-call(bf16[512,2048]{1,0:T(8,128)(2,1)} %tok_hbm.1, bf16[3,2048,512]{2,1,0:T(8,128)(2,1)} %bitcast.2, f32[7,384]{1,0:T(8,128)} %taps_hbm.1, f32[512,128]{1,0:T(8,128)} %filt_hbm.1, f32[1,2048]{1,0:T(1,128)} %bitcast.3, bf16[512,2048]{1,0:T(8,128)(2,1)} %wout_hbm.1, f32[128,64]{1,0:T(8,128)} %constant.8.clone.over_hbm, ...), custom_call_target="tpu_custom_call" | custom-call | tf_op jit(solution)/shard_map/hyena/pallas_call | solution.py:431
  64.5 1.9 %copy.12 = bf16[128,2048]{1,0:T(8,128)(2,1)} copy(bf16[128,2048]{1,0:T(8,128)(2,1)} %hyena.1) | data formatting | bytes 1048576

commit v2 on v1

v2 whole, which is shorter than its diff:
```python
import functools
import math

import jax
import jax.numpy as jnp
import numpy as np
from jax import lax
from jax.experimental import pallas as pl
from jax.experimental.pallas import tpu as pltpu
from jax.sharding import PartitionSpec as P

MESH = pl.DeviceIdType.MESH
F32 = jnp.float32
BF16 = jnp.bfloat16
RIM = 8


def tables(n_ctx, tok_len, stretch):
    blocks = np.arange(n_ctx)
    lags = np.arange(tok_len)
    odd = 2 * blocks + 1
    angle = (odd[:, None] * blocks[None, :] % (4 * n_ctx)) * (2.0 * math.pi / (4 * n_ctx))
    eye = np.eye(stretch)
    over_blocks = np.concatenate([np.cos(angle), -np.sin(angle)], axis=0)
    spread = np.kron(over_blocks, eye)
    turn = (odd[:, None] * lags[None, :]) * (2.0 * math.pi / (4 * n_ctx * tok_len))
    turns = np.stack([np.cos(turn), -np.sin(turn)])
    inner = (lags[:, None] * lags[None, :] % tok_len) * (2.0 * math.pi / tok_len)
    waves = np.concatenate([np.cos(inner), np.sin(inner)], axis=0)
    return (
        over_blocks.astype(np.float32),
        spread.astype(np.float32).astype(jnp.bfloat16),
        turns.astype(np.float32),
        waves.astype(np.float32).astype(jnp.bfloat16),
    )


def dot(a, b, **kw):
    return jnp.dot(a, b, preferred_element_type=F32, **kw)


def kernel(
    n_ctx, n_fft, group_size,
    tok_hbm, w_hbm, taps_hbm, filt_hbm, gain_hbm, wout_hbm, over_hbm, spread_hbm, turns_hbm, waves_hbm,
    kept_out, cross_out,
    tok, w, taps_in, filt, gain_in, wout, over, spread, turns, waves,
    spread_t, proj, mixed, query, send, recv, filt_send, filt_recv,
    signal, lhs, lhs2, spec, back, send2, recv2, gated, part, kept,
    pair_send, pair_recv, cross_send,
    load_sem, rim_send_sem, rim_recv_sem, filt_sem, go_send_sem, go_recv_sem, come_send_sem, come_recv_sem,
    pair_send_sem, pair_recv_sem, cross_send_sem, cross_recv_sem,
):
    me = lax.axis_index("ctx")
    fft = lax.axis_index("fft")
    chip = fft // 2
    core = fft % 2
    partner = chip * 2 + (1 - core)
    across = (1 - chip) * 2 + core
    tok_len, width = tok.shape
    block = w.shape[2]
    stretch = block // n_ctx
    rows = n_ctx * stretch
    n_taps = taps_in.shape[0]
    piece = tok_len // n_fft
    half = tok_len // 2
    tc = min(128, half)
    lc = min(128, block)
    per_lc = lc // stretch

    barrier = pltpu.get_barrier_semaphore()

    def each_peer(act):
        group = next(g for g in (9, 7, 5, 3, 1) if (n_ctx - 1) % g == 0)

        @pl.loop(0, (n_ctx - 1) // group)
        def _(i):
            for j in range(group):
                m = n_ctx - 1 - j - i * group
                d = (m + 1) // 2
                odd = m % 2
                act(lax.rem(me + odd * d + (1 - odd) * (n_ctx - d), n_ctx))

    split = half - 16
    loads = {}
    for slot, (name, src, dst) in enumerate([
        ("taps", taps_hbm, taps_in),
        ("tok1", tok_hbm.at[pl.ds(split, tok_len - split)], tok.at[pl.ds(split, tok_len - split)]),
        ("w1", w_hbm.at[1], w.at[1]), ("w2", w_hbm.at[2], w.at[2]),
        ("filt", filt_hbm, filt), ("tok0", tok_hbm.at[pl.ds(0, split)], tok.at[pl.ds(0, split)]),
        ("w0", w_hbm.at[0], w.at[0]), ("gain", gain_hbm, gain_in),
        ("spread", spread_hbm, spread), ("over", over_hbm, over), ("turns", turns_hbm, turns),
        ("waves", waves_hbm, waves), ("wout", wout_hbm, wout),
    ]):
        loads[name] = pltpu.make_async_copy(src, dst, load_sem.at[slot])
        loads[name].start()
        if name == "w2":
            each_peer(lambda peer: pl.semaphore_signal(barrier, inc=1, device_id={"ctx": peer}, device_id_type=MESH))
            for other in (partner, across, (1 - chip) * 2 + (1 - core)):
                pl.semaphore_signal(barrier, inc=1, device_id={"fft": other}, device_id_type=MESH)

    first_group = fft * (block // group_size)
    per_stream = taps_in.shape[1] // 3
    loads["taps"].wait()
    group_of = lax.broadcasted_iota(jnp.int32, (per_stream, block), 1) // group_size + first_group
    pick = (lax.broadcasted_iota(jnp.int32, (per_stream, block), 0) == group_of).astype(F32)
    blank = jnp.zeros((8 - n_taps, per_stream), F32)
    taps_rows = jnp.concatenate(
        [x for s in range(3) for x in (taps_in[:, s * per_stream:(s + 1) * per_stream], blank)], axis=0
    )
    taps_all = dot(taps_rows, pick, precision=lax.Precision.HIGHEST)

    def project(s, r0, r1):
        for n0 in range(0, block, min(256, block)):
            n1 = n0 + min(256, block)
            got = dot(tok[r0:r1, :], w[s, :, n0:n1])
            proj[s, RIM + r0:RIM + r1, n0:n1] = got.astype(BF16).astype(F32)

    def rim_copy(s):
        return pltpu.make_async_remote_copy(
            src_ref=proj.at[s, pl.ds(tok_len, RIM), :], dst_ref=proj.at[s, pl.ds(0, RIM), :],
            send_sem=rim_send_sem.at[s], recv_sem=rim_recv_sem.at[s],
            device_id={"ctx": lax.rem(me + 1, n_ctx)}, device_id_type=MESH,
        )

    def send_rim(s):
        @pl.when(me < n_ctx - 1)
        def _():
            rim_copy(s).start()

        @pl.when(me == 0)
        def _():
            proj[s, 0:RIM, :] = jnp.zeros((RIM, block), F32)

    def finish_rim(s):
        @pl.when(me > 0)
        def _():
            rim_copy(s).wait_recv()

    def featurize(s, t0, c0):
        window = proj[s, pl.ds(t0, tc + RIM), c0:c0 + lc]
        total = None
        for j in range(n_taps):
            term = taps_all[s * 8 + j:s * 8 + j + 1, c0:c0 + lc] * window[RIM - j:RIM - j + tc, :]
            total = term if total is None else total + term
        return total.astype(BF16).astype(F32)

    def mix(t0, c0):
        both = featurize(1, t0, c0) * featurize(2, t0, c0)
        mixed[pl.ds(t0, tc), c0:c0 + lc] = both
        turned = both.T.reshape(per_lc, stretch, tc).astype(BF16)
        send[c0 // stretch:c0 // stretch + per_lc, :, pl.ds(t0, tc)] = turned

    def exchange(source, target, send_sem, recv_sem):
        def copy_to(dest, h0, size, i):
            return pltpu.make_async_remote_copy(
                src_ref=source.at[dest, :, pl.ds(h0, size)], dst_ref=target.at[me, :, pl.ds(h0, size)],
                send_sem=send_sem.at[i], recv_sem=recv_sem.at[i],
                device_id={"ctx": dest}, device_id_type=MESH,
            )

        def start(h0, size, i):
            each_peer(lambda dest: copy_to(dest, h0, size, i).start())
            target[me, :, pl.ds(h0, size)] = source[me, :, pl.ds(h0, size)]

        def all_of(h0, size, i):
            return pltpu.make_async_remote_copy(
                src_ref=source.at[pl.ds(0, n_ctx - 1), :, pl.ds(h0, size)],
                dst_ref=target.at[pl.ds(0, n_ctx - 1), :, pl.ds(h0, size)],
                send_sem=send_sem.at[i], recv_sem=recv_sem.at[i],
                device_id={"ctx": lax.rem(me + 1, n_ctx)}, device_id_type=MESH,
            )

        return start, all_of

    go_start, go_all = exchange(send, recv, go_send_sem, go_recv_sem)

    loads["tok1"].wait()
    for s, name in ((1, "w1"), (2, "w2")):
        loads[name].wait()
        project(s, split, tok_len)
    for c0 in range(0, block, lc):
        @pl.loop(half // tc, tok_len // tc)
        def _(t):
            mix(pl.multiple_of(t * tc, tc), c0)

    loads["filt"].wait()
    flipped = filt[...].T.astype(BF16).astype(F32)
    lag_rows, lag_lanes = filt_send.shape[1:]
    for j in range(lag_rows):
        filt_send[:, j, :] = flipped[:, j * lag_lanes:(j + 1) * lag_lanes].astype(BF16)

    def filt_copy(dest):
        return pltpu.make_async_remote_copy(
            src_ref=filt_send.at[first_group + (dest * stretch) // group_size],
            dst_ref=filt_recv.at[me],
            send_sem=filt_sem.at[0], recv_sem=filt_sem.at[1],
            device_id={"ctx": dest}, device_id_type=MESH,
        )

    filt_all = pltpu.make_async_remote_copy(
        src_ref=filt_recv.at[pl.ds(0, n_ctx - 1)], dst_ref=filt_recv.at[pl.ds(0, n_ctx - 1)],
        send_sem=filt_sem.at[0], recv_sem=filt_sem.at[1],
        device_id={"ctx": lax.rem(me + 1, n_ctx)}, device_id_type=MESH,
    )
    filt_recv[me] = filt_send[first_group + (me * stretch) // group_size]

    pl.semaphore_wait(barrier, n_ctx - 1 + 3)
    send_rim(1)
    send_rim(2)
    go_start(half, half, 1)
    each_peer(lambda dest: filt_copy(dest).start())

    loads["tok0"].wait()
    project(1, 0, split)
    project(2, 0, split)
    for c0 in range(0, block, lc):
        @pl.loop(1, half // tc)
        def _(t):
            mix(pl.multiple_of(t * tc, tc), c0)

    finish_rim(1)
    finish_rim(2)
    for c0 in range(0, block, lc):
        mix(0, c0)
    go_start(0, half, 0)

    loads["w0"].wait()
    project(0, 0, tok_len)
    send_rim(0)
    loads["spread"].wait()
    spread_t[...] = spread[...].T

    kc = min(8, n_ctx)
    kr = kc * stretch
    mc = min(256, rows)

    def turned_by(table, re, im, m0, cols):
        n = re.shape[1]
        re = re.reshape(-1, stretch, n)
        im = im.reshape(-1, stretch, n)
        k0 = m0 // stretch
        b_re = table[0, k0:k0 + re.shape[0], cols][:, None, :]
        b_im = table[1, k0:k0 + re.shape[0], cols][:, None, :]
        return re, im, b_re, b_im

    loads["turns"].wait()

    def first_stage(h0):
        @pl.loop(0, n_ctx // kc)
        def _(i):
            got = recv[pl.ds(i * kc, kc), :, h0:h0 + half].astype(F32)
            signal[pl.ds(pl.multiple_of(i * kr, kr), kr), h0:h0 + half] = got.reshape(kr, half).astype(BF16)

        for m0 in range(0, rows, mc):
            re, im, b_re, b_im = turned_by(
                turns, dot(spread[m0:m0 + mc, :], signal[:, h0:h0 + half]),
                dot(spread[rows + m0:rows + m0 + mc, :], signal[:, h0:h0 + half]), m0, pl.ds(h0, half))
            o_re = (re * b_re - im * b_im).reshape(mc, half)
            o_im = (re * b_im + im * b_re).reshape(mc, half)
            lhs[m0:m0 + mc, h0:h0 + half] = o_re.astype(BF16)
            lhs[m0:m0 + mc, tok_len + h0:tok_len + h0 + half] = o_im.astype(BF16)
            lhs[rows + m0:rows + m0 + mc, h0:h0 + half] = o_im.astype(BF16)
            lhs[rows + m0:rows + m0 + mc, tok_len + h0:tok_len + h0 + half] = (-o_re).astype(BF16)

    loads["over"].wait()
    loads["waves"].wait()
    filt_all.wait_recv()
    lags3 = filt_recv[...].astype(F32)
    lags = jnp.concatenate([lags3[:, j, :] for j in range(lag_rows)], axis=1).astype(BF16)
    first = dot(over[...].astype(BF16), lags)
    f_re, f_im = first[:n_ctx], first[n_ctx:]
    t_re, t_im = turns[0], turns[1]
    g_re = (f_re * t_re - f_im * t_im).astype(BF16)
    g_im = (f_re * t_im + f_im * t_re).astype(BF16)
    top = jnp.concatenate([g_re, g_im], axis=1)
    bottom = jnp.concatenate([g_im, -g_re], axis=1)
    scale = 1.0 / (n_ctx * tok_len)
    spec[0] = dot(top, waves[...]) * scale
    spec[1] = dot(bottom, waves[...]) * scale

    go_all(half, half, 1).wait_recv()
    first_stage(half)

    go_all(0, half, 0).wait_recv()
    first_stage(0)

    for m0 in range(0, rows, mc):
        re, im, b_re, b_im = turned_by(
            spec, dot(lhs[m0:m0 + mc, :], waves[...]), dot(lhs[rows + m0:rows + m0 + mc, :], waves[...]),
            m0, slice(None))
        o_re = (re * b_re - im * b_im).reshape(mc, tok_len)
        o_im = (re * b_im + im * b_re).reshape(mc, tok_len)
        lhs2[m0:m0 + mc, :tok_len] = o_re.astype(BF16)
        lhs2[m0:m0 + mc, tok_len:] = (-o_im).astype(BF16)
        lhs2[rows + m0:rows + m0 + mc, :tok_len] = o_im.astype(BF16)
        lhs2[rows + m0:rows + m0 + mc, tok_len:] = o_re.astype(BF16)

    come_start, come_all = exchange(send2, recv2, come_send_sem, come_recv_sem)

    def last_stage(h0):
        cols = pl.ds(h0, half)
        for m0 in range(0, rows, mc):
            re, im, b_re, b_im = turned_by(
                turns, dot(lhs2[m0:m0 + mc, :], waves[:, cols]),
                dot(lhs2[rows + m0:rows + m0 + mc, :], waves[:, cols]), m0, cols)
            back[m0:m0 + mc, :] = (re * b_re + im * b_im).reshape(mc, half).astype(BF16)
            back[rows + m0:rows + m0 + mc, :] = (im * b_re - re * b_im).reshape(mc, half).astype(BF16)

        for m0 in range(0, rows, mc):
            got = dot(spread_t[m0:m0 + mc, :], back[...])
            send2[m0 // stretch:(m0 + mc) // stretch, :, cols] = (
                got.reshape(mc // stretch, stretch, half).astype(BF16))

    theirs = (1 - chip) * half
    ours = pl.multiple_of(chip * half, half)
    parts = [pl.multiple_of(theirs + j * piece, piece) for j in range(2)]
    last_stage(pl.multiple_of(theirs, half))
    come_start(parts[0], piece, 0)
    come_start(parts[1], piece, 1)
    last_stage(ours)
    come_start(ours, half, 2)

    finish_rim(0)
    for c0 in range(0, block, lc):
        @pl.loop(0, tok_len // tc)
        def _(t):
            t0 = pl.multiple_of(t * tc, tc)
            query[pl.ds(t0, tc), c0:c0 + lc] = featurize(0, t0, c0)

    loads["wout"].wait()
    loads["gain"].wait()
    gain_row = gain_in[:, pl.ds(pl.multiple_of(fft * block, block), block)]
    n_chunks, oc = part.shape[0], part.shape[2]
    share = n_chunks // 2
    gc = min(128, piece)

    def gate(h0, size):
        for c0 in range(0, block, lc):
            for t in range(0, size, gc):
                t0 = pl.multiple_of(h0 + t, gc)
                got = recv2[c0 // stretch:c0 // stretch + per_lc, :, pl.ds(t0, gc)].astype(F32)
                conv = got.reshape(lc, gc).T
                whole = conv + gain_row[:, c0:c0 + lc] * mixed[pl.ds(t0, gc), c0:c0 + lc]
                gated[pl.ds(t0, gc), c0:c0 + lc] = (query[pl.ds(t0, gc), c0:c0 + lc] * whole).astype(BF16)

    def pair_copy(n):
        return pltpu.make_async_remote_copy(
            src_ref=pair_send.at[n], dst_ref=pair_recv.at[n],
            send_sem=pair_send_sem.at[n], recv_sem=pair_recv_sem.at[n],
            device_id={"fft": partner}, device_id_type=MESH,
        )

    def cross_copy(j, i):
        n = core * share + i
        return pltpu.make_async_remote_copy(
            src_ref=cross_send.at[j, i], dst_ref=cross_out.at[:, pl.ds(pl.multiple_of(n * oc, oc), oc)],
            send_sem=cross_send_sem.at[j, i], recv_sem=cross_recv_sem.at[n],
            device_id={"fft": (1 - chip) * 2 + j}, device_id_type=MESH,
        )

    def cross_arrival(n):
        return pltpu.make_async_remote_copy(
            src_ref=cross_send.at[0, 0], dst_ref=cross_out.at[:, n * oc:(n + 1) * oc],
            send_sem=cross_send_sem.at[0, 0], recv_sem=cross_recv_sem.at[n],
            device_id={"fft": across}, device_id_type=MESH,
        )

    def product(h0, size, n):
        return dot(gated[pl.ds(h0, size), :], wout[:, pl.ds(pl.multiple_of(n * oc, oc), oc)])

    go_all(half, half, 1).wait_send()
    go_all(0, half, 0).wait_send()
    filt_all.wait_send()

    @pl.when(me < n_ctx - 1)
    def _():
        for s in range(3):
            rim_copy(s).wait_send()

    for j in range(2):
        come_all(parts[j], piece, j).wait_recv()
        gate(parts[j], piece)
        for i in range(share):
            pair_send[j * share + i] = product(parts[j], piece, (1 - core) * share + i).astype(BF16)
            pair_copy(j * share + i).start()
        for i in range(share):
            part[i, 0:piece, :] = product(parts[j], piece, core * share + i)
        for i in range(share):
            pair_copy(j * share + i).wait_recv()
            cross_send[j, i] = (part[i, 0:piece, :] + pair_recv[j * share + i].astype(F32)).astype(BF16)
            cross_copy(j, i).start()

    come_all(ours, half, 2).wait_recv()
    gate(ours, half)
    for n in range(n_chunks):
        part[n] = product(ours, half, n)
        other = part[n, pl.ds(pl.multiple_of((1 - core) * piece, piece), piece), :]
        pair_send[n_chunks + n] = other.astype(BF16)
        pair_copy(n_chunks + n).start()
    for n in range(n_chunks):
        pair_copy(n_chunks + n).wait_recv()
        mine = part[n, pl.ds(pl.multiple_of(core * piece, piece), piece), :]
        kept[:, n * oc:(n + 1) * oc] = mine + pair_recv[n_chunks + n].astype(F32)
    keep = pltpu.make_async_copy(kept, kept_out, load_sem.at[0])
    keep.start()

    come_all(parts[0], piece, 0).wait_send()
    come_all(parts[1], piece, 1).wait_send()
    come_all(ours, half, 2).wait_send()
    for n in range(2 * n_chunks):
        pair_copy(n).wait_send()
    keep.wait()
    for n in range(n_chunks):
        cross_arrival(n).wait_recv()
    for j in range(2):
        for i in range(share):
            cross_copy(j, i).wait_send()


def body(tokens, w_in, short_taps, long_filter, skip_gain, w_out):
    n_ctx = lax.axis_size("ctx")
    n_fft = lax.axis_size("fft")
    tok_len, width = tokens.shape
    block = w_in.shape[2]
    n_groups = long_filter.shape[1]
    group_size = width // n_groups
    stretch = block // n_ctx
    rows = n_ctx * stretch
    piece = tok_len // n_fft
    oc = min(512, width // 4)
    n_chunks = width // oc
    lag_rows = 4
    over, spread, turns, waves = tables(n_ctx, tok_len, stretch)
    dma = pltpu.SemaphoreType.DMA
    vmem = pltpu.VMEM
    streams = w_in.transpose(1, 0, 2)
    args = (
        tokens, streams, short_taps, long_filter, skip_gain.reshape(1, width), w_out,
        jnp.asarray(over), jnp.asarray(spread), jnp.asarray(turns), jnp.asarray(waves),
    )
    kept, crossed = pl.pallas_call(
        functools.partial(kernel, n_ctx, n_fft, group_size),
        out_shape=(jax.ShapeDtypeStruct((piece, width), F32), jax.ShapeDtypeStruct((piece, width), BF16)),
        in_specs=[pl.BlockSpec(memory_space=pl.ANY)] * len(args),
        out_specs=(pl.BlockSpec(memory_space=pl.ANY), pl.BlockSpec(memory_space=pl.ANY)),
        scratch_shapes=[vmem(a.shape, a.dtype) for a in args] + [
            vmem((rows, 2 * rows), BF16),
            vmem((3, tok_len + RIM, block), F32),
            vmem((tok_len, block), F32),
            vmem((tok_len, block), F32),
            vmem((n_ctx, stretch, tok_len), BF16),
            vmem((n_ctx, stretch, tok_len), BF16),
            vmem((n_groups, lag_rows, tok_len // lag_rows), BF16),
            vmem((n_ctx, lag_rows, tok_len // lag_rows), BF16),
            vmem((rows, tok_len), BF16),
            vmem((2 * rows, 2 * tok_len), BF16),
            vmem((2 * rows, 2 * tok_len), BF16),
            vmem((2, n_ctx, tok_len), F32),
            vmem((2 * rows, tok_len // 2), BF16),
            vmem((n_ctx, stretch, tok_len), BF16),
            vmem((n_ctx, stretch, tok_len), BF16),
            vmem((tok_len, block), BF16),
            vmem((n_chunks, tok_len // 2, oc), F32),
            vmem((piece, width), F32),
            vmem((2 * n_chunks, piece, oc), BF16),
            vmem((2 * n_chunks, piece, oc), BF16),
            vmem((2, n_chunks // 2, piece, oc), BF16),
            dma((13,)), dma((3,)), dma((3,)), dma((2,)), dma((2,)), dma((2,)), dma((3,)), dma((3,)),
            dma((2 * n_chunks,)), dma((2 * n_chunks,)), dma((2, n_chunks // 2)), dma((n_chunks,)),
        ],
        compiler_params=pltpu.CompilerParams(
            collective_id=0, has_side_effects=True, vmem_limit_bytes=60 * 1024 * 1024
        ),
        name="hyena",
    )(*args)
    return (kept + crossed.astype(F32)).astype(BF16)


def solution(mesh):
    return jax.shard_map(
        body,
        mesh=mesh,
        in_specs=(P("ctx", None), P(None, None, "fft"), P(), P("ctx", None), P(), P("fft", None)),
        out_specs=P(("ctx", "fft"), None),
        check_vma=False,
    )
```

time: 66.6 us -> 60.3 us (0.905)
  Pallas kernels: 64.5 us -> 57.9 us
  other arithmetic: 0 us -> 2.26 us
  local copies, waits for them, and re-layouts: 1.88 us -> 0 us
    pallas_call x1, Pallas kernels: 64.5 us -> 57.9 us  [body(): pl.pallas_call(functools.partial(kernel, n_ctx, n_fft, group_size), out_s...]
    convert_element_type x0 -> x1, other arithmetic: none -> 2.26 us  [body(): return (kept + crossed.astype(F32)).astype(BF16)]
    unnamed x1 -> x0, local copies, waits for them, and re-layouts: 1.88 us -> none
where the time goes in v2:
time: 60.3 us; the launch traced here: 60.2 us
  Pallas kernels  57.9 us (96%)
  other arithmetic  2.26 us (4%)
    pallas_call x1, Pallas kernels, body(): pl.pallas_call(functools.partial(kernel, n_ctx, n_fft, group_size), out_s...  57.9 us
    convert_element_type x1, other arithmetic, body(): return (kept + crossed.astype(F32)).astype(BF16)  2.26 us

profile of v2, /device:TPU:1, one launch (start us, length us, event | category | flops | bytes accessed | tf_op | source)
XLA Modules:
  0.0 60.2 jit_solution(15917327678599179049)
XLA Ops:
  0.0 57.9 %hyena.1 = (f32[128,2048]{1,0:T(8,128)}, bf16[128,2048]{1,0:T(8,128)(2,1)}) custom-call(bf16[512,2048]{1,0:T(8,128)(2,1)} %tok_hbm.1, bf16[3,2048,512]{2,1,0:T(8,128)(2,1)} %bitcast.2, f32[7,384]{1,0:T(8,128)} %taps_hbm.1, f32[512,128]{1,0:T(8,128)} %filt_hbm.1, f32[1,2048]{1,0:T(1,128)} %bitcast.3, bf16[512,2048]{1,0:T(8,128)(2,1)} %wout_hbm.1, ...), custom_call_target="tpu_custom_call" | custom-call | tf_op jit(solution)/shard_map/hyena/pallas_call | solution.py:441
  57.9 2.3 %add_convert_fusion = bf16[128,2048]{1,0:T(8,128)(2,1)} fusion(f32[128,2048]{1,0:T(8,128)} %get-tuple-element.7, bf16[128,2048]{1,0:T(8,128)(2,1)} %get-tuple-element.8), kind=kLoop, calls=%fused_computation | loop fusion | flops 786432 | bytes 2097152 | tf_op jit(solution)/shard_map/convert_element_type | solution.py:476

commit v3 on v2

--- a/solution.py
+++ b/solution.py
@@ -46,14 +46,15 @@
     tok, w, taps_in, filt, gain_in, wout, over, spread, turns, waves,
     spread_t, proj, mixed, query, send, recv, filt_send, filt_recv,
     signal, lhs, lhs2, spec, back, send2, recv2, gated, part, kept,
-    pair_send, pair_recv, cross_send,
+    pair_send, pair_recv, cross_send, twin_query, twin_mixed,
     load_sem, rim_send_sem, rim_recv_sem, filt_sem, go_send_sem, go_recv_sem, come_send_sem, come_recv_sem,
-    pair_send_sem, pair_recv_sem, cross_send_sem, cross_recv_sem,
+    pair_send_sem, pair_recv_sem, cross_send_sem, cross_recv_sem, twin_sem,
 ):
     me = lax.axis_index("ctx")
     fft = lax.axis_index("fft")
     chip = fft // 2
     core = fft % 2
+    twin = me + 1 - 2 * (me % 2)
     partner = chip * 2 + (1 - core)
     across = (1 - chip) * 2 + core
     tok_len, width = tok.shape
@@ -97,6 +98,9 @@
             each_peer(lambda peer: pl.semaphore_signal(barrier, inc=1, device_id={"ctx": peer}, device_id_type=MESH))
             for other in (partner, across, (1 - chip) * 2 + (1 - core)):
                 pl.semaphore_signal(barrier, inc=1, device_id={"fft": other}, device_id_type=MESH)
+            for k in range(2):
+                pl.semaphore_signal(
+                    barrier, inc=1, device_id={"ctx": twin, "fft": (1 - chip) * 2 + k}, device_id_type=MESH)
 
     first_group = fft * (block // group_size)
     per_stream = taps_in.shape[1] // 3
@@ -113,11 +117,13 @@
         for n0 in range(0, block, min(256, block)):
             n1 = n0 + min(256, block)
             got = dot(tok[r0:r1, :], w[s, :, n0:n1])
-            proj[s, RIM + r0:RIM + r1, n0:n1] = got.astype(BF16).astype(F32)
+            got = got.astype(BF16).astype(F32)
+            for c0 in range(n0, n1, lc):
+                proj[s, c0 // lc, RIM + r0:RIM + r1, :] = got[:, c0 - n0:c0 - n0 + lc]
 
     def rim_copy(s):
         return pltpu.make_async_remote_copy(
-            src_ref=proj.at[s, pl.ds(tok_len, RIM), :], dst_ref=proj.at[s, pl.ds(0, RIM), :],
+            src_ref=proj.at[s, :, pl.ds(tok_len, RIM), :], dst_ref=proj.at[s, :, pl.ds(0, RIM), :],
             send_sem=rim_send_sem.at[s], recv_sem=rim_recv_sem.at[s],
             device_id={"ctx": lax.rem(me + 1, n_ctx)}, device_id_type=MESH,
         )
@@ -129,7 +135,7 @@
 
         @pl.when(me == 0)
         def _():
-            proj[s, 0:RIM, :] = jnp.zeros((RIM, block), F32)
+            proj[s, :, 0:RIM, :] = jnp.zeros((block // lc, RIM, lc), F32)
 
     def finish_rim(s):
         @pl.when(me > 0)
@@ -137,10 +143,9 @@
             rim_copy(s).wait_recv()
 
     def featurize(s, t0, c0):
-        window = proj[s, pl.ds(t0, tc + RIM), c0:c0 + lc]
         total = None
         for j in range(n_taps):
-            term = taps_all[s * 8 + j:s * 8 + j + 1, c0:c0 + lc] * window[RIM - j:RIM - j + tc, :]
+            term = taps_all[s * 8 + j:s * 8 + j + 1, c0:c0 + lc] * proj[s, c0 // lc, pl.ds(t0 + (RIM - j), tc), :]
             total = term if total is None else total + term
         return total.astype(BF16).astype(F32)
 
@@ -151,16 +156,20 @@
         send[c0 // stretch:c0 // stretch + per_lc, :, pl.ds(t0, tc)] = turned
 
     def exchange(source, target, send_sem, recv_sem):
-        def copy_to(dest, h0, size, i):
+        def held_for(dest, crossed):
+            return dest + 1 - 2 * (dest % 2) if crossed else dest
+
+        def copy_to(dest, h0, size, i, crossed):
             return pltpu.make_async_remote_copy(
-                src_ref=source.at[dest, :, pl.ds(h0, size)], dst_ref=target.at[me, :, pl.ds(h0, size)],
+                src_ref=source.at[held_for(dest, crossed), :, pl.ds(h0, size)],
+                dst_ref=target.at[me, :, pl.ds(h0, size)],
                 send_sem=send_sem.at[i], recv_sem=recv_sem.at[i],
                 device_id={"ctx": dest}, device_id_type=MESH,
             )
 
-        def start(h0, size, i):
-            each_peer(lambda dest: copy_to(dest, h0, size, i).start())
-            target[me, :, pl.ds(h0, size)] = source[me, :, pl.ds(h0, size)]
+        def start(h0, size, i, crossed=False):
+            each_peer(lambda dest: copy_to(dest, h0, size, i, crossed).start())
+            target[me, :, pl.ds(h0, size)] = source[held_for(me, crossed), :, pl.ds(h0, size)]
 
         def all_of(h0, size, i):
             return pltpu.make_async_remote_copy(
@@ -204,7 +213,7 @@
     )
     filt_recv[me] = filt_send[first_group + (me * stretch) // group_size]
 
-    pl.semaphore_wait(barrier, n_ctx - 1 + 3)
+    pl.semaphore_wait(barrier, n_ctx - 1 + 3 + 2)
     send_rim(1)
     send_rim(2)
     go_start(half, half, 1)
@@ -281,6 +290,29 @@
     go_all(half, half, 1).wait_recv()
     first_stage(half)
 
+    finish_rim(0)
+    for c0 in range(0, block, lc):
+        @pl.loop(0, tok_len // tc)
+        def _(t):
+            t0 = pl.multiple_of(t * tc, tc)
+            query[pl.ds(t0, tc), c0:c0 + lc] = featurize(0, t0, c0).astype(BF16)
+
+    theirs = (1 - chip) * half
+    ours = pl.multiple_of(chip * half, half)
+    parts = [pl.multiple_of(theirs + j * piece, piece) for j in range(2)]
+    twin_mixed[0] = mixed[pl.ds(parts[1], piece), :].astype(BF16)
+
+    def twin_copy(i):
+        return pltpu.make_async_remote_copy(
+            src_ref=(query.at[pl.ds(parts[1], piece)], twin_mixed.at[0])[i],
+            dst_ref=(twin_query, twin_mixed.at[1])[i],
+            send_sem=twin_sem.at[0, i], recv_sem=twin_sem.at[1, i],
+            device_id={"ctx": twin}, device_id_type=MESH,
+        )
+
+    twin_copy(0).start()
+    twin_copy(1).start()
+
     go_all(0, half, 0).wait_recv()
     first_stage(0)
 
@@ -297,35 +329,25 @@
 
     come_start, come_all = exchange(send2, recv2, come_send_sem, come_recv_sem)
 
-    def last_stage(h0):
-        cols = pl.ds(h0, half)
+    def last_stage(h0, size):
+        cols = pl.ds(h0, size)
         for m0 in range(0, rows, mc):
             re, im, b_re, b_im = turned_by(
                 turns, dot(lhs2[m0:m0 + mc, :], waves[:, cols]),
                 dot(lhs2[rows + m0:rows + m0 + mc, :], waves[:, cols]), m0, cols)
-            back[m0:m0 + mc, :] = (re * b_re + im * b_im).reshape(mc, half).astype(BF16)
-            back[rows + m0:rows + m0 + mc, :] = (im * b_re - re * b_im).reshape(mc, half).astype(BF16)
+            back[m0:m0 + mc, :size] = (re * b_re + im * b_im).reshape(mc, size).astype(BF16)
+            back[rows + m0:rows + m0 + mc, :size] = (im * b_re - re * b_im).reshape(mc, size).astype(BF16)
 
         for m0 in range(0, rows, mc):
-            got = dot(spread_t[m0:m0 + mc, :], back[...])
+            got = dot(spread_t[m0:m0 + mc, :], back[:, :size])
             send2[m0 // stretch:(m0 + mc) // stretch, :, cols] = (
-                got.reshape(mc // stretch, stretch, half).astype(BF16))
-
-    theirs = (1 - chip) * half
-    ours = pl.multiple_of(chip * half, half)
-    parts = [pl.multiple_of(theirs + j * piece, piece) for j in range(2)]
-    last_stage(pl.multiple_of(theirs, half))
-    come_start(parts[0], piece, 0)
-    come_start(parts[1], piece, 1)
-    last_stage(ours)
+                got.reshape(mc // stretch, stretch, size).astype(BF16))
+
+    for j in range(2):
+        last_stage(parts[j], piece)
+        come_start(parts[j], piece, j, crossed=j == 1)
+    last_stage(ours, half)
     come_start(ours, half, 2)
-
-    finish_rim(0)
-    for c0 in range(0, block, lc):
-        @pl.loop(0, tok_len // tc)
-        def _(t):
-            t0 = pl.multiple_of(t * tc, tc)
-            query[pl.ds(t0, tc), c0:c0 + lc] = featurize(0, t0, c0)
 
     loads["wout"].wait()
     loads["gain"].wait()
@@ -334,14 +356,16 @@
     share = n_chunks // 2
     gc = min(128, piece)
 
-    def gate(h0, size):
+    def gate(h0, size, asked, direct, off):
         for c0 in range(0, block, lc):
             for t in range(0, size, gc):
                 t0 = pl.multiple_of(h0 + t, gc)
                 got = recv2[c0 // stretch:c0 // stretch + per_lc, :, pl.ds(t0, gc)].astype(F32)
                 conv = got.reshape(lc, gc).T
-                whole = conv + gain_row[:, c0:c0 + lc] * mixed[pl.ds(t0, gc), c0:c0 + lc]
-                gated[pl.ds(t0, gc), c0:c0 + lc] = (query[pl.ds(t0, gc), c0:c0 + lc] * whole).astype(BF16)
+                at = pl.multiple_of(off + t, gc)
+                whole = conv + gain_row[:, c0:c0 + lc] * direct[pl.ds(at, gc), c0:c0 + lc].astype(F32)
+                gated[pl.ds(t0, gc), c0:c0 + lc] = (
+                    asked[pl.ds(at, gc), c0:c0 + lc].astype(F32) * whole).astype(BF16)
 
     def pair_copy(n):
         return pltpu.make_async_remote_copy(
@@ -355,7 +379,7 @@
         return pltpu.make_async_remote_copy(
             src_ref=cross_send.at[j, i], dst_ref=cross_out.at[:, pl.ds(pl.multiple_of(n * oc, oc), oc)],
             send_sem=cross_send_sem.at[j, i], recv_sem=cross_recv_sem.at[n],
-            device_id={"fft": (1 - chip) * 2 + j}, device_id_type=MESH,
+            device_id={"ctx": twin if j else me, "fft": (1 - chip) * 2 + j}, device_id_type=MESH,
         )
 
     def cross_arrival(n):
@@ -379,7 +403,12 @@
 
     for j in range(2):
         come_all(parts[j], piece, j).wait_recv()
-        gate(parts[j], piece)
+        if j == 0:
+            gate(parts[j], piece, query, mixed, parts[j])
+        else:
+            twin_copy(0).wait_recv()
+            twin_copy(1).wait_recv()
+            gate(parts[j], piece, twin_query, twin_mixed.at[1], 0)
         for i in range(share):
             pair_send[j * share + i] = product(parts[j], piece, (1 - core) * share + i).astype(BF16)
             pair_copy(j * share + i).start()
@@ -391,7 +420,7 @@
             cross_copy(j, i).start()
 
     come_all(ours, half, 2).wait_recv()
-    gate(ours, half)
+    gate(ours, half, query, mixed, ours)
     for n in range(n_chunks):
         part[n] = product(ours, half, n)
         other = part[n, pl.ds(pl.multiple_of((1 - core) * piece, piece), piece), :]
@@ -410,6 +439,8 @@
     for n in range(2 * n_chunks):
         pair_copy(n).wait_send()
     keep.wait()
+    twin_copy(0).wait_send()
+    twin_copy(1).wait_send()
     for n in range(n_chunks):
         cross_arrival(n).wait_recv()
     for j in range(2):
@@ -430,6 +461,7 @@
     oc = min(512, width // 4)
     n_chunks = width // oc
     lag_rows = 4
+    lc = min(128, block)
     over, spread, turns, waves = tables(n_ctx, tok_len, stretch)
     dma = pltpu.SemaphoreType.DMA
     vmem = pltpu.VMEM
@@ -445,9 +477,9 @@
         out_specs=(pl.BlockSpec(memory_space=pl.ANY), pl.BlockSpec(memory_space=pl.ANY)),
         scratch_shapes=[vmem(a.shape, a.dtype) for a in args] + [
             vmem((rows, 2 * rows), BF16),
-            vmem((3, tok_len + RIM, block), F32),
+            vmem((3, block // lc, tok_len + RIM, lc), F32),
             vmem((tok_len, block), F32),
-            vmem((tok_len, block), F32),
+            vmem((tok_len, block), BF16),
             vmem((n_ctx, stretch, tok_len), BF16),
             vmem((n_ctx, stretch, tok_len), BF16),
             vmem((n_groups, lag_rows, tok_len // lag_rows), BF16),
@@ -465,8 +497,10 @@
             vmem((2 * n_chunks, piece, oc), BF16),
             vmem((2 * n_chunks, piece, oc), BF16),
             vmem((2, n_chunks // 2, piece, oc), BF16),
+            vmem((piece, block), BF16),
+            vmem((2, piece, block), BF16),
             dma((13,)), dma((3,)), dma((3,)), dma((2,)), dma((2,)), dma((2,)), dma((3,)), dma((3,)),
-            dma((2 * n_chunks,)), dma((2 * n_chunks,)), dma((2, n_chunks // 2)), dma((n_chunks,)),
+            dma((2 * n_chunks,)), dma((2 * n_chunks,)), dma((2, n_chunks // 2)), dma((n_chunks,)), dma((2, 2)),
         ],
         compiler_params=pltpu.CompilerParams(
             collective_id=0, has_side_effects=True, vmem_limit_bytes=60 * 1024 * 1024

time: 60.3 us -> 57.1 us (0.947)
  Pallas kernels: 57.9 us -> 54.8 us
    pallas_call x1, Pallas kernels: 57.9 us -> 54.8 us  [body(): pl.pallas_call(functools.partial(kernel, n_ctx, n_fft, group_size), out_s...]
where the time goes in v3:
time: 57.1 us; the launch traced here: 57 us
  Pallas kernels  54.8 us (96%)
  other arithmetic  2.26 us (4%)
    pallas_call x1, Pallas kernels, body(): pl.pallas_call(functools.partial(kernel, n_ctx, n_fft, group_size), out_s...  54.8 us
    convert_element_type x1, other arithmetic, body(): return (kept + crossed.astype(F32)).astype(BF16)  2.26 us

profile of v3, /device:TPU:1, one launch (start us, length us, event | category | flops | bytes accessed | tf_op | source)
XLA Modules:
  0.0 57.0 jit_solution(17321137140073779524)
XLA Ops:
  0.0 54.8 %hyena.1 = (f32[128,2048]{1,0:T(8,128)}, bf16[128,2048]{1,0:T(8,128)(2,1)}) custom-call(bf16[512,2048]{1,0:T(8,128)(2,1)} %tok_hbm.1, bf16[3,2048,512]{2,1,0:T(8,128)(2,1)} %bitcast.2, f32[7,384]{1,0:T(8,128)} %taps_hbm.1, f32[512,128]{1,0:T(8,128)} %filt_hbm.1, f32[1,2048]{1,0:T(1,128)} %bitcast.3, bf16[512,2048]{1,0:T(8,128)(2,1)} %wout_hbm.1, ...), custom_call_target="tpu_custom_call" | custom-call | tf_op jit(solution)/shard_map/hyena/pallas_call | solution.py:473
  54.8 2.3 %add_convert_fusion = bf16[128,2048]{1,0:T(8,128)(2,1)} fusion(f32[128,2048]{1,0:T(8,128)} %get-tuple-element.7, bf16[128,2048]{1,0:T(8,128)(2,1)} %get-tuple-element.8), kind=kLoop, calls=%fused_computation | loop fusion | flops 786432 | bytes 2097152 | tf_op jit(solution)/shard_map/convert_element_type | solution.py:510

commit v4 on v3

--- a/solution.py
+++ b/solution.py
@@ -71,15 +71,23 @@
     barrier = pltpu.get_barrier_semaphore()
 
     def each_peer(act):
-        group = next(g for g in (9, 7, 5, 3, 1) if (n_ctx - 1) % g == 0)
-
-        @pl.loop(0, (n_ctx - 1) // group)
-        def _(i):
-            for j in range(group):
-                m = n_ctx - 1 - j - i * group
-                d = (m + 1) // 2
-                odd = m % 2
-                act(lax.rem(me + odd * d + (1 - odd) * (n_ctx - d), n_ctx))
+        def around(offset):
+            peer = me + offset
+            return jnp.where(peer >= n_ctx, peer - n_ctx, peer)
+
+        far = n_ctx // 2
+        group = next(g for g in (5, 3, 1) if (far - 2) % g == 0)
+        act(around(far))
+        act(around(far - 1))
+        act(around(n_ctx - far + 1))
+
+        if far > 2:
+            @pl.loop(0, (far - 2) // group)
+            def _(i):
+                for j in range(group):
+                    d = far - 2 - j - i * group
+                    act(around(d))
+                    act(around(n_ctx - d))
 
     split = half - 16
     loads = {}
@@ -192,6 +200,11 @@
         def _(t):
             mix(pl.multiple_of(t * tc, tc), c0)
 
+    pl.semaphore_wait(barrier, n_ctx - 1 + 3 + 2)
+    send_rim(1)
+    send_rim(2)
+    go_start(half, half, 1)
+
     loads["filt"].wait()
     flipped = filt[...].T.astype(BF16).astype(F32)
     lag_rows, lag_lanes = filt_send.shape[1:]
@@ -212,11 +225,6 @@
         device_id={"ctx": lax.rem(me + 1, n_ctx)}, device_id_type=MESH,
     )
     filt_recv[me] = filt_send[first_group + (me * stretch) // group_size]
-
-    pl.semaphore_wait(barrier, n_ctx - 1 + 3 + 2)
-    send_rim(1)
-    send_rim(2)
-    go_start(half, half, 1)
     each_peer(lambda dest: filt_copy(dest).start())
 
     loads["tok0"].wait()
@@ -413,10 +421,12 @@
             pair_send[j * share + i] = product(parts[j], piece, (1 - core) * share + i).astype(BF16)
             pair_copy(j * share + i).start()
         for i in range(share):
-            part[i, 0:piece, :] = product(parts[j], piece, core * share + i)
+            part[i, j * piece:(j + 1) * piece, :] = product(parts[j], piece, core * share + i)
+    for j in range(2):
         for i in range(share):
             pair_copy(j * share + i).wait_recv()
-            cross_send[j, i] = (part[i, 0:piece, :] + pair_recv[j * share + i].astype(F32)).astype(BF16)
+            mine = part[i, j * piece:(j + 1) * piece, :]
+            cross_send[j, i] = (mine + pair_recv[j * share + i].astype(F32)).astype(BF16)
             cross_copy(j, i).start()
 
     come_all(ours, half, 2).wait_recv()
@@ -429,7 +439,7 @@
     for n in range(n_chunks):
         pair_copy(n_chunks + n).wait_recv()
         mine = part[n, pl.ds(pl.multiple_of(core * piece, piece), piece), :]
-        kept[:, n * oc:(n + 1) * oc] = mine + pair_recv[n_chunks + n].astype(F32)
+        kept[:, n * oc:(n + 1) * oc] = (mine + pair_recv[n_chunks + n].astype(F32)).astype(BF16)
     keep = pltpu.make_async_copy(kept, kept_out, load_sem.at[0])
     keep.start()
 
@@ -472,7 +482,7 @@
     )
     kept, crossed = pl.pallas_call(
         functools.partial(kernel, n_ctx, n_fft, group_size),
-        out_shape=(jax.ShapeDtypeStruct((piece, width), F32), jax.ShapeDtypeStruct((piece, width), BF16)),
+        out_shape=(jax.ShapeDtypeStruct((piece, width), BF16), jax.ShapeDtypeStruct((piece, width), BF16)),
         in_specs=[pl.BlockSpec(memory_space=pl.ANY)] * len(args),
         out_specs=(pl.BlockSpec(memory_space=pl.ANY), pl.BlockSpec(memory_space=pl.ANY)),
         scratch_shapes=[vmem(a.shape, a.dtype) for a in args] + [
@@ -493,7 +503,7 @@
             vmem((n_ctx, stretch, tok_len), BF16),
             vmem((tok_len, block), BF16),
             vmem((n_chunks, tok_len // 2, oc), F32),
-            vmem((piece, width), F32),
+            vmem((piece, width), BF16),
             vmem((2 * n_chunks, piece, oc), BF16),
             vmem((2 * n_chunks, piece, oc), BF16),
             vmem((2, n_chunks // 2, piece, oc), BF16),
@@ -507,7 +517,7 @@
         ),
         name="hyena",
     )(*args)
-    return (kept + crossed.astype(F32)).astype(BF16)
+    return (kept.astype(F32) + crossed.astype(F32)).astype(BF16)
 
 
 def solution(mesh):

time: 57.1 us -> 57 us (level)
  no operation moved by 1% of the time
where the time goes in v4:
time: 57 us; the launch traced here: 56.8 us
  Pallas kernels  54.7 us (96%)
  other arithmetic  2.12 us (4%)
    pallas_call x1, Pallas kernels, body(): pl.pallas_call(functools.partial(kernel, n_ctx, n_fft, group_size), out_s...  54.7 us
    convert_element_type x1, other arithmetic, body(): return (kept.astype(F32) + crossed.astype(F32)).astype(BF16)  2.12 us

profile of v4, /device:TPU:1, one launch (start us, length us, event | category | flops | bytes accessed | tf_op | source)
XLA Modules:
  0.0 56.8 jit_solution(5676255802545242342)
XLA Ops:
  0.0 54.7 %hyena.1 = (bf16[128,2048]{1,0:T(8,128)(2,1)}, bf16[128,2048]{1,0:T(8,128)(2,1)}) custom-call(bf16[512,2048]{1,0:T(8,128)(2,1)} %tok_hbm.1, bf16[3,2048,512]{2,1,0:T(8,128)(2,1)} %bitcast.2, f32[7,384]{1,0:T(8,128)} %taps_hbm.1, f32[512,128]{1,0:T(8,128)} %filt_hbm.1, f32[1,2048]{1,0:T(1,128)} %bitcast.3, bf16[512,2048]{1,0:T(8,128)(2,1)} %wout_hbm.1, ...), custom_call_target="tpu_custom_call" | custom-call | tf_op jit(solution)/shard_map/hyena/pallas_call | solution.py:483
  54.7 2.1 %add_convert_fusion = bf16[128,2048]{1,0:T(8,128)(2,1)} fusion(bf16[128,2048]{1,0:T(8,128)(2,1)} %get-tuple-element.8, bf16[128,2048]{1,0:T(8,128)(2,1)} %get-tuple-element.7), kind=kLoop, calls=%fused_computation | loop fusion | flops 1048576 | bytes 1572864 | tf_op jit(solution)/shard_map/convert_element_type | solution.py:520

commit v5 on v4

--- a/solution.py
+++ b/solution.py
@@ -157,8 +157,11 @@
             total = term if total is None else total + term
         return total.astype(BF16).astype(F32)
 
+    def keys(t0, c0):
+        mixed[pl.ds(t0, tc), c0:c0 + lc] = featurize(1, t0, c0)
+
     def mix(t0, c0):
-        both = featurize(1, t0, c0) * featurize(2, t0, c0)
+        both = mixed[pl.ds(t0, tc), c0:c0 + lc] * featurize(2, t0, c0)
         mixed[pl.ds(t0, tc), c0:c0 + lc] = both
         turned = both.T.reshape(per_lc, stretch, tc).astype(BF16)
         send[c0 // stretch:c0 // stretch + per_lc, :, pl.ds(t0, tc)] = turned
@@ -195,10 +198,10 @@
     for s, name in ((1, "w1"), (2, "w2")):
         loads[name].wait()
         project(s, split, tok_len)
-    for c0 in range(0, block, lc):
-        @pl.loop(half // tc, tok_len // tc)
-        def _(t):
-            mix(pl.multiple_of(t * tc, tc), c0)
+        for c0 in range(0, block, lc):
+            @pl.loop(half // tc, tok_len // tc)
+            def _(t):
+                (keys if s == 1 else mix)(pl.multiple_of(t * tc, tc), c0)
 
     pl.semaphore_wait(barrier, n_ctx - 1 + 3 + 2)
     send_rim(1)
@@ -233,11 +236,13 @@
     for c0 in range(0, block, lc):
         @pl.loop(1, half // tc)
         def _(t):
+            keys(pl.multiple_of(t * tc, tc), c0)
             mix(pl.multiple_of(t * tc, tc), c0)
 
     finish_rim(1)
     finish_rim(2)
     for c0 in range(0, block, lc):
+        keys(0, c0)
         mix(0, c0)
     go_start(0, half, 0)
 
@@ -298,13 +303,6 @@
     go_all(half, half, 1).wait_recv()
     first_stage(half)
 
-    finish_rim(0)
-    for c0 in range(0, block, lc):
-        @pl.loop(0, tok_len // tc)
-        def _(t):
-            t0 = pl.multiple_of(t * tc, tc)
-            query[pl.ds(t0, tc), c0:c0 + lc] = featurize(0, t0, c0).astype(BF16)
-
     theirs = (1 - chip) * half
     ours = pl.multiple_of(chip * half, half)
     parts = [pl.multiple_of(theirs + j * piece, piece) for j in range(2)]
@@ -318,7 +316,6 @@
             device_id={"ctx": twin}, device_id_type=MESH,
         )
 
-    twin_copy(0).start()
     twin_copy(1).start()
 
     go_all(0, half, 0).wait_recv()
@@ -351,10 +348,17 @@
             send2[m0 // stretch:(m0 + mc) // stretch, :, cols] = (
                 got.reshape(mc // stretch, stretch, size).astype(BF16))
 
+    last_stage(pl.multiple_of(theirs, half), half)
     for j in range(2):
-        last_stage(parts[j], piece)
         come_start(parts[j], piece, j, crossed=j == 1)
     last_stage(ours, half)
+    finish_rim(0)
+    for c0 in range(0, block, lc):
+        @pl.loop(0, tok_len // tc)
+        def _(t):
+            t0 = pl.multiple_of(t * tc, tc)
+            query[pl.ds(t0, tc), c0:c0 + lc] = featurize(0, t0, c0).astype(BF16)
+    twin_copy(0).start()
     come_start(ours, half, 2)
 
     loads["wout"].wait()

time: 57 us -> 56.4 us (0.989)
  Pallas kernels: 54.7 us -> 54.1 us
    pallas_call x1, Pallas kernels: 54.7 us -> 54.1 us  [body(): pl.pallas_call(functools.partial(kernel, n_ctx, n_fft, group_size), out_s...]
where the time goes in v5:
time: 56.4 us; the launch traced here: 56.2 us
  Pallas kernels  54.1 us (96%)
  other arithmetic  2.12 us (4%)
    pallas_call x1, Pallas kernels, body(): pl.pallas_call(functools.partial(kernel, n_ctx, n_fft, group_size), out_s...  54.1 us
    convert_element_type x1, other arithmetic, body(): return (kept.astype(F32) + crossed.astype(F32)).astype(BF16)  2.12 us

profile of v5, /device:TPU:1, one launch (start us, length us, event | category | flops | bytes accessed | tf_op | source)
XLA Modules:
  0.0 56.2 jit_solution(12958987180353817710)
XLA Ops:
  0.0 54.1 %hyena.1 = (bf16[128,2048]{1,0:T(8,128)(2,1)}, bf16[128,2048]{1,0:T(8,128)(2,1)}) custom-call(bf16[512,2048]{1,0:T(8,128)(2,1)} %tok_hbm.1, bf16[3,2048,512]{2,1,0:T(8,128)(2,1)} %bitcast.2, f32[7,384]{1,0:T(8,128)} %taps_hbm.1, f32[512,128]{1,0:T(8,128)} %filt_hbm.1, f32[1,2048]{1,0:T(1,128)} %bitcast.3, bf16[512,2048]{1,0:T(8,128)(2,1)} %wout_hbm.1, ...), custom_call_target="tpu_custom_call" | custom-call | tf_op jit(solution)/shard_map/hyena/pallas_call | solution.py:487
  54.1 2.1 %add_convert_fusion = bf16[128,2048]{1,0:T(8,128)(2,1)} fusion(bf16[128,2048]{1,0:T(8,128)(2,1)} %get-tuple-element.8, bf16[128,2048]{1,0:T(8,128)(2,1)} %get-tuple-element.7), kind=kLoop, calls=%fused_computation | loop fusion | flops 1048576 | bytes 1572864 | tf_op jit(solution)/shard_map/convert_element_type | solution.py:524
